TPU v7x, 32 devices: a whole 2x2x4 slice. The times are simulated.
32 devices in a mesh: dp: 8 (over z, y), ctx: 4 (over x, core).
Axes of the slice: x: 2, y: 2, z: 4, core: 2. Of those that a mesh axis runs over, the one named last changes fastest.
Arguments:
- hidden_in: float32 [4096, 1024], P(('dp', 'ctx')), may hold values from -6 to 6
- positions: int32 [4096], P(('dp', 'ctx')), may hold values from 0 to 511, as said below
- mixer_params: float32 [32, 197760], P(('dp', 'ctx'))
- feed_params: float32 [32, 196736], P(('dp', 'ctx'))
- mixer_first: float32 [32, 197760], P(('dp', 'ctx')), may hold values from -96 to 96
- feed_first: float32 [32, 196736], P(('dp', 'ctx')), may hold values from -96 to 96
- mixer_second: float32 [32, 197760], P(('dp', 'ctx')), may hold values from 256 to 16384
- feed_second: float32 [32, 196736], P(('dp', 'ctx')), may hold values from 256 to 16384
- out_grad: float32 [4096, 1024], P(('dp', 'ctx')), may hold values from -6 to 6
Outputs:
- block_out: float32 [4096, 1024], P(('dp', 'ctx'))
- grad_input: float32 [4096, 1024], P(('dp', 'ctx'))
- mixer_grad: float32 [32, 197760], P(('dp', 'ctx'))
- feed_grad: float32 [32, 196736], P(('dp', 'ctx'))
- mixer_new: float32 [32, 197760], P(('dp', 'ctx'))
- feed_new: float32 [32, 196736], P(('dp', 'ctx'))
- mixer_first_new: float32 [32, 197760], P(('dp', 'ctx'))
- feed_first_new: float32 [32, 196736], P(('dp', 'ctx'))
- mixer_second_new: float32 [32, 197760], P(('dp', 'ctx'))
- feed_second_new: float32 [32, 196736], P(('dp', 'ctx'))
Inputs may be any that keep to these rules, and one draw needn't show every extreme that they name: `positions`: each entry is 0 where a sequence starts and one more than the entry before it otherwise; every block of 512 rows starts a sequence at its first row; sequences hold at most 512 tokens and lengths vary.
All inputs are finite; a program needn't handle non-finite values.
Results may differ from a plain program's by a relative error of at most 0.019.
The roundings to bfloat16 on the way count: a program that leaves them out, or rounds other values in their place, can miss the bound.
Values may be sent and summed in bfloat16 or wider, within the bound.
No kernel may reach another device: no remote copies, remote signals or barrier semaphores. Data moves between devices by JAX's collectives and lax.ppermute only.
A program may use at most 384 MiB of HBM per device.

v0:
```python
from functools import partial
import math

import jax
import jax.numpy as jnp
from jax import lax
from jax.sharding import PartitionSpec as P

D = 1024
FF = 2048
HEADS_SSM = 24
HEAD_SSM = 64
STATE = 128
KERNEL = 4
HEADS = 8
KV_HEADS = 2
HD = 64
STEP = 10
DI = 1536
CONV_COLS = 1792
QUERY_CHANNELS = 512
KEY_CHANNELS = 128
IN_COLS = 3352
QKV_COLS = 768


eps_norm = 1e-05
rope_base = 100000000000.0
neg_large = -1e30
beta_one = 0.9
beta_two = 0.95
learn_rate = 0.01
decay_weight = 0.1
adam_eps = 1e-08
highest = lax.Precision.HIGHEST


def passed_along(shard, axis, by):
    length = lax.axis_size(axis)
    pairs = [(i, i + by) for i in range(length) if 0 <= i + by < length]
    return lax.ppermute(shard, axis, pairs)


def entering(part, axis, combine, identity):
    place = lax.axis_index(axis)
    gathered = jax.tree.map(lambda a: lax.all_gather(a, axis), part)
    state = jax.tree.map(lambda a, e: jnp.zeros_like(a) + jnp.asarray(e, a.dtype), part, identity)

    def one(step, state):
        return combine(
            state, jax.tree.map(lambda a: lax.dynamic_index_in_dim(a, step, 0, False), gathered)
        )

    return lax.fori_loop(0, place, one, state)


def entering_2(shard, axis, combine, identity):
    length, position = (lax.axis_size(axis), lax.axis_index(axis))
    everything = jax.tree.map(
        lambda part, kind: lax.all_gather(part.astype(kind), axis),
        shard,
        jax.tree.map(lambda a: jnp.bfloat16 if a.dtype == jnp.float32 else a.dtype, shard),
    )
    start = jax.tree.map(
        lambda part, zero: jnp.broadcast_to(jnp.asarray(zero, part.dtype), part.shape),
        shard,
        identity,
    )

    def step(k, before):
        at = length - 1 - k
        reached = at > position
        new = combine(
            before, jax.tree.map(lambda part, own: part[at].astype(own.dtype), everything, shard)
        )
        return jax.tree.map(lambda a, b: jnp.where(reached, a, b), new, before)

    return lax.fori_loop(0, length, step, start)


def rms_norm(values, gain_vec):
    return (
        values * lax.rsqrt(jnp.mean(values * values, axis=-1, keepdims=True) + eps_norm) * gain_vec
    )


def swiglu(gate_up):
    return jax.nn.silu(gate_up[:, :FF]) * gate_up[:, FF:]


def gate_product(ssm_out, ssm_gate):
    return ssm_out * jax.nn.silu(ssm_gate)


def causal_conv(positions, extended, conv_weight, conv_bias):
    row_count = positions.shape[0]
    summed = jnp.broadcast_to(conv_bias[None, :], (row_count, conv_bias.shape[0]))
    for tap_index in range(KERNEL):
        first_row = KERNEL - 1 - tap_index
        earlier = extended[first_row : first_row + row_count]
        usable = (positions >= tap_index).astype(jnp.float32)[:, None]
        summed = summed + usable * earlier * conv_weight[tap_index][None, :]
    return jax.nn.silu(summed)


def mixer_layouts():
    return [
        (D, IN_COLS),
        (DI, D),
        (D, QKV_COLS),
        (QUERY_CHANNELS, D),
        (KERNEL, CONV_COLS),
        (CONV_COLS,),
        (D,),
        (HEADS_SSM,),
        (HEADS_SSM,),
        (HEADS_SSM,),
    ]


def feed_layouts():
    return [(D, 2 * FF), (FF, D), (D,)]


def unflatten(flat, layouts):
    result = []
    cursor = 0
    for layout in layouts:
        length = math.prod(layout)
        result.append(flat[cursor : cursor + length].reshape(layout))
        cursor = cursor + length
    return result


def pack_rows(pieces, devices, width):
    members = [member.reshape(-1) for member in pieces]
    filled = sum((member.shape[0] for member in members))
    members.append(jnp.zeros((devices * width - filled,), jnp.float32))
    return jnp.concatenate(members).reshape(devices, width)


def rope_tables(positions):
    half_dim = HD // 2
    frequency = jnp.exp(-jnp.log(rope_base) * jnp.arange(half_dim, dtype=jnp.float32) * 2.0 / HD)
    angles = positions.astype(jnp.float32)[:, None] * frequency[None, :]
    return (jnp.cos(angles), jnp.sin(angles))


def apply_rotary(values, cosine_table, sine_table, reverse):
    row_count = values.shape[0]
    half_dim = HD // 2
    per_head = values.reshape(row_count, -1, HD)
    first_half = per_head[..., :half_dim]
    second_half = per_head[..., half_dim:]
    cos_wide = cosine_table[:, None, :]
    sin_wide = sine_table[:, None, :]
    if reverse:
        rotated = jnp.concatenate(
            [
                first_half * cos_wide + second_half * sin_wide,
                second_half * cos_wide - first_half * sin_wide,
            ],
            axis=-1,
        )
    else:
        rotated = jnp.concatenate(
            [
                first_half * cos_wide - second_half * sin_wide,
                second_half * cos_wide + first_half * sin_wide,
            ],
            axis=-1,
        )
    return rotated.reshape(row_count, -1)


def attention_mask(positions, offset, key_count):
    query_index = offset + jnp.arange(positions.shape[0], dtype=jnp.int32)
    key_index = jnp.arange(key_count, dtype=jnp.int32)
    return (key_index[None, :] <= query_index[:, None]) & (
        key_index[None, :] >= (query_index - positions)[:, None]
    )


def attend(queries, key_tile_rows, value_tile_rows, allowed):
    row_count = queries.shape[0]
    group_size = HEADS // KV_HEADS
    query_head_rows = queries.reshape(row_count, KV_HEADS, group_size, HD)
    key_heads = key_tile_rows.reshape(-1, KV_HEADS, HD)
    value_heads = value_tile_rows.reshape(-1, KV_HEADS, HD)
    scores = jnp.einsum(
        "rkgd,skd->kgrs", query_head_rows, key_heads, preferred_element_type=jnp.float32
    ) * HD ** (-0.5)
    unnormed = jnp.exp(jnp.where(allowed[None, None], scores, neg_large))
    row_sum = jnp.sum(unnormed, axis=-1, keepdims=True)
    mixed = (
        jnp.einsum(
            "kgrs,skd->kgrd",
            unnormed.astype(jnp.bfloat16),
            value_heads,
            preferred_element_type=jnp.float32,
        )
        / row_sum
    )
    attended = jnp.transpose(mixed, (2, 0, 1, 3)).reshape(row_count, QUERY_CHANNELS)
    log_total = jnp.log(row_sum[..., 0])
    return (attended, log_total)


def attend_back(
    queries, key_tile_rows, value_tile_rows, attended_b, grad_att_b, log_total, allowed
):
    row_count = queries.shape[0]
    group_size = HEADS // KV_HEADS
    query_head_rows = queries.reshape(row_count, KV_HEADS, group_size, HD)
    key_heads = key_tile_rows.reshape(-1, KV_HEADS, HD)
    value_heads = value_tile_rows.reshape(-1, KV_HEADS, HD)
    scores = jnp.einsum(
        "rkgd,skd->kgrs", query_head_rows, key_heads, preferred_element_type=jnp.float32
    ) * HD ** (-0.5)
    probs = jnp.exp(jnp.where(allowed[None, None], scores - log_total[..., None], neg_large))
    gradient_heads = grad_att_b.reshape(row_count, KV_HEADS, group_size, HD)
    out_heads = attended_b.reshape(row_count, KV_HEADS, group_size, HD)
    grad_probs = jnp.einsum(
        "rkgd,skd->kgrs", gradient_heads, value_heads, preferred_element_type=jnp.float32
    )
    row_dot = jnp.transpose(
        jnp.sum(gradient_heads.astype(jnp.float32) * out_heads.astype(jnp.float32), axis=-1),
        (1, 2, 0),
    )
    gradient_scores = (probs * (grad_probs - row_dot[..., None]) * HD ** (-0.5)).astype(
        jnp.bfloat16
    )
    grad_queries = jnp.einsum(
        "kgrs,skd->rkgd", gradient_scores, key_heads, preferred_element_type=jnp.float32
    ).reshape(row_count, QUERY_CHANNELS)
    gradient_keys = jnp.einsum(
        "hxbe,bhxo->eho", gradient_scores, query_head_rows, preferred_element_type=jnp.float32
    ).reshape(-1, KEY_CHANNELS)
    gradient_values = jnp.einsum(
        "hxbe,bhxo->eho",
        probs.astype(jnp.bfloat16),
        gradient_heads,
        preferred_element_type=jnp.float32,
    ).reshape(-1, KEY_CHANNELS)
    return (grad_queries, gradient_keys, gradient_values)


def span_decays(step_raw, bias_step, log_rate):
    step_size = jax.nn.softplus(step_raw + bias_step[None, :])
    cumulative = jnp.cumsum(-jnp.exp(log_rate)[None, :] * step_size, axis=0)
    return (step_size, cumulative)


def scaled_input(ssm_input, step_size):
    row_count = ssm_input.shape[0]
    return ssm_input.reshape(row_count, HEADS_SSM, HEAD_SSM) * step_size[:, :, None]


def span_summary(segment, ssm_input, state_write, step_raw, bias_step, log_rate):
    step_size, cumulative = span_decays(step_raw, bias_step, log_rate)
    weighted = scaled_input(ssm_input, step_size)
    same_end = (segment == segment[-1]).astype(jnp.float32)
    end_weight = same_end[:, None] * jnp.exp(cumulative[-1][None, :] - cumulative)
    local_state = jnp.einsum("sh,shp,sn->hpn", end_weight, weighted, state_write, precision=highest)
    total_decay = jnp.exp(cumulative[-1]) * (segment[-1] == 0).astype(jnp.float32)
    return (total_decay, local_state)


def span_apply(
    segment, ssm_input, state_write, state_read, step_raw, bias_step, log_rate, skip_gain, state_in
):
    step_size, cumulative = span_decays(step_raw, bias_step, log_rate)
    weighted = scaled_input(ssm_input, step_size)
    row_count = ssm_input.shape[0]
    row_order = jnp.arange(row_count, dtype=jnp.int32)
    allowed = (row_order[None, :] <= row_order[:, None]) & (segment[None, :] == segment[:, None])
    log_gaps = cumulative[:, None, :] - cumulative[None, :, :]
    decay_pairs = jnp.exp(jnp.where(allowed[:, :, None], log_gaps, neg_large))
    read_write = jnp.dot(state_read, state_write.T, precision=highest)
    inner_part = jnp.einsum(
        "tsh,shp->thp", read_write[:, :, None] * decay_pairs, weighted, precision=highest
    )
    carried = (segment == 0).astype(jnp.float32)[:, None] * jnp.exp(cumulative)
    from_state = (
        jnp.einsum("tn,hpn->thp", state_read, state_in, precision=highest) * carried[:, :, None]
    )
    skip_part = skip_gain[None, :, None] * ssm_input.reshape(row_count, HEADS_SSM, HEAD_SSM)
    return (inner_part + from_state + skip_part).reshape(row_count, DI)


def span_full(
    segment, ssm_input, state_write, state_read, step_raw, bias_step, log_rate, skip_gain, state_in
):
    total_decay, local_state = span_summary(
        segment, ssm_input, state_write, step_raw, bias_step, log_rate
    )
    output = span_apply(
        segment,
        ssm_input,
        state_write,
        state_read,
        step_raw,
        bias_step,
        log_rate,
        skip_gain,
        state_in,
    )
    return (output, total_decay[:, None, None] * state_in + local_state)


def span_direct(segment, state_read, step_raw, bias_step, log_rate, grad_out):
    step_size, cumulative = span_decays(step_raw, bias_step, log_rate)
    row_count = grad_out.shape[0]
    carried = (segment == 0).astype(jnp.float32)[:, None] * jnp.exp(cumulative)
    weighted_grad = grad_out.reshape(row_count, HEADS_SSM, HEAD_SSM) * carried[:, :, None]
    return jnp.einsum("thp,tn->hpn", weighted_grad, state_read, precision=highest)


def combine_states(before_part, after_part):
    return (
        before_part[0] * after_part[0],
        after_part[0][:, None, None] * before_part[1] + after_part[1],
    )


def sources_first(parts):
    return tuple((jnp.sum(member, axis=0, keepdims=True) for member in parts))


def adam_step(weights, grads, first_state, second_state):
    first_next = beta_one * first_state + (1.0 - beta_one) * grads
    second_next = beta_two * second_state + (1.0 - beta_two) * grads * grads
    first_hat = first_next / (1.0 - beta_one**STEP)
    second_hat = second_next / (1.0 - beta_two**STEP)
    weight_next = weights - learn_rate * (
        first_hat / (jnp.sqrt(second_hat) + adam_eps) + decay_weight * weights
    )
    return (weight_next, first_next, second_next)


def body(
    hidden_in,
    positions,
    mixer_params,
    feed_params,
    mixer_first,
    feed_first,
    mixer_second,
    feed_second,
    out_grad,
):
    devices = lax.axis_size(("dp", "ctx"))
    block_count = lax.axis_size("dp")
    piece_count = lax.axis_size("ctx")
    mixer_width = mixer_params.shape[1]
    feed_width = feed_params.shape[1]
    mixer_all, feed_all = (
        lax.all_gather(mixer_params.astype(jnp.bfloat16), ("dp", "ctx"), axis=0, tiled=True),
        lax.all_gather(feed_params.astype(jnp.bfloat16), ("dp", "ctx"), axis=0, tiled=True),
    )
    (
        w_in,
        w_ssm_out,
        w_qkv,
        w_attn_out,
        conv_weight,
        conv_bias,
        gain_one,
        bias_step,
        log_rate,
        skip_gain,
    ) = unflatten(mixer_all.reshape(-1), mixer_layouts())
    w_gate_up, w_down, gain_two = unflatten(feed_all.reshape(-1), feed_layouts())
    bias_step = bias_step.astype(jnp.float32)
    log_rate = log_rate.astype(jnp.float32)
    skip_gain = skip_gain.astype(jnp.float32)
    row_count = hidden_in.shape[0]
    normed_one, norm_one_back = jax.vjp(rms_norm, hidden_in, gain_one.astype(jnp.float32))
    normed_b = normed_one.astype(jnp.bfloat16)
    projected = jnp.dot(normed_b, w_in, preferred_element_type=jnp.float32)
    ssm_gate = projected[:, :DI]
    conv_input = projected[:, DI : DI + CONV_COLS]
    step_raw = projected[:, DI + CONV_COLS :]
    rim_rows = passed_along(conv_input[row_count - (KERNEL - 1) :], "ctx", 1)
    extended = jnp.concatenate([rim_rows, conv_input], axis=0)
    conv_out, conv_back = jax.vjp(
        partial(causal_conv, positions),
        extended,
        conv_weight.astype(jnp.float32),
        conv_bias.astype(jnp.float32),
    )
    ssm_input = conv_out[:, :DI]
    state_write = conv_out[:, DI : DI + STATE]
    state_read = conv_out[:, DI + STATE :]
    segment = jnp.cumsum((positions == 0).astype(jnp.int32))
    total_decay, local_state = span_summary(
        segment, ssm_input, state_write, step_raw, bias_step, log_rate
    )
    identity = (jnp.ones_like(total_decay), jnp.zeros_like(local_state))
    _, state_in = entering((total_decay, local_state), "ctx", combine_states, identity)
    ssm_out = span_apply(
        segment,
        ssm_input,
        state_write,
        state_read,
        step_raw,
        bias_step,
        log_rate,
        skip_gain,
        state_in,
    )
    gated, gate_back = jax.vjp(gate_product, ssm_out, ssm_gate)
    gated_b = gated.astype(jnp.bfloat16)
    mamba_branch = jnp.dot(gated_b, w_ssm_out, preferred_element_type=jnp.float32)
    query_key_value = jnp.dot(normed_b, w_qkv, preferred_element_type=jnp.float32)
    cosine_table, sine_table = rope_tables(positions)
    queries = apply_rotary(
        query_key_value[:, :QUERY_CHANNELS], cosine_table, sine_table, False
    ).astype(jnp.bfloat16)
    key_segment_rows = apply_rotary(
        query_key_value[:, QUERY_CHANNELS : QUERY_CHANNELS + KEY_CHANNELS],
        cosine_table,
        sine_table,
        False,
    ).astype(jnp.bfloat16)
    value_segment_rows = query_key_value[:, QUERY_CHANNELS + KEY_CHANNELS :].astype(jnp.bfloat16)
    key_tile_rows, value_tile_rows = (
        lax.all_gather(key_segment_rows, "ctx", axis=0, tiled=True),
        lax.all_gather(value_segment_rows, "ctx", axis=0, tiled=True),
    )
    offset = lax.axis_index("ctx") * row_count
    allowed = attention_mask(positions, offset, key_tile_rows.shape[0])
    attended, log_total = attend(queries, key_tile_rows, value_tile_rows, allowed)
    attended_b = attended.astype(jnp.bfloat16)
    attn_branch = jnp.dot(attended_b, w_attn_out, preferred_element_type=jnp.float32)
    residual = hidden_in + mamba_branch + attn_branch
    normed_two, norm_two_back = jax.vjp(rms_norm, residual, gain_two.astype(jnp.float32))
    normed_two_b = normed_two.astype(jnp.bfloat16)
    gate_up = jnp.dot(normed_two_b, w_gate_up, preferred_element_type=jnp.float32)
    activated, swiglu_back = jax.vjp(swiglu, gate_up)
    activated_b = activated.astype(jnp.bfloat16)
    block_out = residual + jnp.dot(activated_b, w_down, preferred_element_type=jnp.float32)
    grad_b = out_grad.astype(jnp.bfloat16)
    grad_w_down = jnp.dot(activated_b.T, grad_b, preferred_element_type=jnp.float32)
    grad_activated = jnp.dot(grad_b, w_down.T, preferred_element_type=jnp.float32)
    grad_gate_up = swiglu_back(grad_activated)[0].astype(jnp.bfloat16)
    grad_w_gate_up = jnp.dot(normed_two_b.T, grad_gate_up, preferred_element_type=jnp.float32)
    grad_normed_two = jnp.dot(grad_gate_up, w_gate_up.T, preferred_element_type=jnp.float32)
    grad_resid_mlp, grad_gain_two = norm_two_back(grad_normed_two)
    grad_residual = out_grad + grad_resid_mlp
    feed_grads = (grad_w_gate_up, grad_w_down, grad_gain_two)
    grad_mix_b = grad_residual.astype(jnp.bfloat16)
    grad_w_ssm_out = jnp.dot(gated_b.T, grad_mix_b, preferred_element_type=jnp.float32)
    grad_gated = jnp.dot(grad_mix_b, w_ssm_out.T, preferred_element_type=jnp.float32)
    grad_ssm_out, grad_ssm_gate = gate_back(grad_gated)
    direct = span_direct(segment, state_read, step_raw, bias_step, log_rate, grad_ssm_out)
    _, grad_state_end = entering_2((total_decay, direct), "ctx", combine_states, identity)
    _, span_back = jax.vjp(
        partial(span_full, segment),
        ssm_input,
        state_write,
        state_read,
        step_raw,
        bias_step,
        log_rate,
        skip_gain,
        state_in,
    )
    grad_in, grad_write, grad_read, grad_step, grad_bias, grad_rate, grad_skip, _ = span_back(
        (grad_ssm_out, grad_state_end)
    )
    grad_extended, grad_conv_weight, grad_conv_bias = conv_back(
        jnp.concatenate([grad_in, grad_write, grad_read], axis=1)
    )
    rim_grads = passed_along(grad_extended[: KERNEL - 1], "ctx", -1)
    grad_conv_input = jnp.concatenate(
        [grad_extended[KERNEL - 1 : row_count], grad_extended[row_count:] + rim_grads], axis=0
    )
    grad_projected = jnp.concatenate([grad_ssm_gate, grad_conv_input, grad_step], axis=1).astype(
        jnp.bfloat16
    )
    grad_w_attn_out = jnp.dot(attended_b.T, grad_mix_b, preferred_element_type=jnp.float32)
    grad_att_b = jnp.dot(grad_mix_b, w_attn_out.T, preferred_element_type=jnp.float32).astype(
        jnp.bfloat16
    )
    grad_queries, grad_key_block, grad_value_block = attend_back(
        queries, key_tile_rows, value_tile_rows, attended_b, grad_att_b, log_total, allowed
    )
    gradient_keys, gradient_values = (
        lax.psum_scatter(
            grad_key_block.astype(jnp.bfloat16), "ctx", scatter_dimension=0, tiled=True
        ).astype(jnp.float32),
        lax.psum_scatter(
            grad_value_block.astype(jnp.bfloat16), "ctx", scatter_dimension=0, tiled=True
        ).astype(jnp.float32),
    )
    grad_qkv = jnp.concatenate(
        [
            apply_rotary(grad_queries, cosine_table, sine_table, True),
            apply_rotary(gradient_keys, cosine_table, sine_table, True),
            gradient_values,
        ],
        axis=1,
    ).astype(jnp.bfloat16)
    grad_w_qkv = jnp.dot(normed_b.T, grad_qkv, preferred_element_type=jnp.float32)
    grad_w_in = jnp.dot(normed_b.T, grad_projected, preferred_element_type=jnp.float32)
    grad_normed_one = jnp.dot(grad_projected, w_in.T, preferred_element_type=jnp.float32) + jnp.dot(
        grad_qkv, w_qkv.T, preferred_element_type=jnp.float32
    )
    grad_resid_norm, grad_gain_one = norm_one_back(grad_normed_one)
    grad_input = grad_residual + grad_resid_norm
    mixer_grads = (
        grad_w_in,
        grad_w_ssm_out,
        grad_w_qkv,
        grad_w_attn_out,
        grad_conv_weight,
        grad_conv_bias,
        grad_gain_one,
        grad_bias,
        grad_rate,
        grad_skip,
    )
    mixer_rows = pack_rows(mixer_grads, devices, mixer_width).reshape(
        block_count, piece_count, mixer_width
    )
    feed_rows = pack_rows(feed_grads, devices, feed_width).reshape(
        block_count, piece_count, feed_width
    )
    mixer_block, feed_block = sources_first(
        (
            lax.all_to_all(
                mixer_rows.astype(jnp.bfloat16), "dp", split_axis=0, concat_axis=0, tiled=True
            ).astype(mixer_rows.dtype),
            lax.all_to_all(
                feed_rows.astype(jnp.bfloat16), "dp", split_axis=0, concat_axis=0, tiled=True
            ).astype(feed_rows.dtype),
        )
    )
    mixer_owned, feed_owned = (
        lax.psum_scatter(
            mixer_block.astype(jnp.bfloat16), "ctx", scatter_dimension=1, tiled=True
        ).astype(jnp.float32),
        lax.psum_scatter(
            feed_block.astype(jnp.bfloat16), "ctx", scatter_dimension=1, tiled=True
        ).astype(jnp.float32),
    )
    mixer_grad = mixer_owned.reshape(1, mixer_width)
    feed_grad = feed_owned.reshape(1, feed_width)
    mixer_new, mixer_first_new, mixer_second_new = adam_step(
        mixer_params, mixer_grad, mixer_first, mixer_second
    )
    feed_new, feed_first_new, feed_second_new = adam_step(
        feed_params, feed_grad, feed_first, feed_second
    )
    return (
        block_out,
        grad_input,
        mixer_grad,
        feed_grad,
        mixer_new,
        feed_new,
        mixer_first_new,
        feed_first_new,
        mixer_second_new,
        feed_second_new,
    )


def solution(mesh):
    in_specs = (
        P(("dp", "ctx"), None),
        P(("dp", "ctx")),
        P(("dp", "ctx"), None),
        P(("dp", "ctx"), None),
        P(("dp", "ctx"), None),
        P(("dp", "ctx"), None),
        P(("dp", "ctx"), None),
        P(("dp", "ctx"), None),
        P(("dp", "ctx"), None),
    )
    out_specs = (
        P(("dp", "ctx"), None),
        P(("dp", "ctx"), None),
        P(("dp", "ctx"), None),
        P(("dp", "ctx"), None),
        P(("dp", "ctx"), None),
        P(("dp", "ctx"), None),
        P(("dp", "ctx"), None),
        P(("dp", "ctx"), None),
        P(("dp", "ctx"), None),
        P(("dp", "ctx"), None),
    )
    return jax.shard_map(body, mesh=mesh, in_specs=in_specs, out_specs=out_specs, check_vma=False)
```

profile of v0, /device:TPU:0, one launch (start us, length us, event | category | flops | bytes accessed | tf_op | source)
XLA Modules:
  0.0 1552.1 jit_solution(992505243426087448)
XLA Ops:
  13.6 155.3 %all-gather.15.cloned.1.call-done = bf16[32,1,197760]{2,1,0:T(2,128)(2,1)} async-done(((bf16[1,1,197760]{2,1,0:T(2,128)(2,1)}), bf16[32,1,197760]{2,1,0:T(2,128)(2,1)}) %all-gather.15.cloned.1.call-update) | async-done | bytes 12656656 | tf_op jit(solution)/shard_map/all_gather | solution.py:358
  168.9 76.8 %reduce.5 = bf16[32,197760]{1,0:T(8,128)(2,1)} reduce(bf16[32,1,197760]{2,1,0:T(2,128)(2,1)} %all-gather.15.cloned.1.call-done, bf16[]{:T(256)} %constant.202), dimensions={1}, to_apply=%all-gather.2.reduce_sub_computation | reduce | bytes 25313282 | tf_op jit(solution)/shard_map/all_gather | solution.py:358
  245.7 22.5 %reshape.594 = bf16[6328320]{0:T(1024)(128)(2,1)} reshape(bf16[32,197760]{1,0:T(8,128)(2,1)} %reduce.5) | data formatting | bytes 25313280 | tf_op jit(solution)/shard_map/reshape | solution.py:372
  268.2 6.2 slice.212
  274.5 13.4 reshape.595
  289.3 5.8 fusion.171
  309.7 14.9 all-gather.17.cloned.1.call-done
  324.6 268.1 %reduce.8 = bf16[32,196736]{1,0:T(8,128)(2,1)} reduce(bf16[32,1,196736]{2,1,0:T(2,128)(2,1)} %all-gather.17.cloned.1.call-done, bf16[]{:T(256)} %constant.202), dimensions={1}, to_apply=%all-gather.4.reduce_sub_computation | reduce | bytes 25182210 | tf_op jit(solution)/shard_map/all_gather | solution.py:359
  592.7 22.8 %reshape.604 = bf16[6295552]{0:T(1024)(128)(2,1)} reshape(bf16[32,196736]{1,0:T(8,128)(2,1)} %reduce.8) | data formatting | bytes 25182208 | tf_op jit(solution)/shard_map/reshape | solution.py:373
  615.5 26.4 %slice.200 = bf16[6148,1024]{1,0:T(8,128)(2,1)} reshape(bf16[32,196736]{1,0:T(8,128)(2,1)} %reduce.8) | data formatting | bytes 25182208 | tf_op jit(solution)/shard_map/slice | solution.py:130
  641.9 18.9 %slice.196 = bf16[1537,4096]{1,0:T(8,128)(2,1)} reshape(bf16[32,196736]{1,0:T(8,128)(2,1)} %reduce.8) | data formatting | bytes 25182208 | tf_op jit(solution)/shard_map/slice | solution.py:130
  662.1 28.1 %slice.184 = bf16[6180,1024]{1,0:T(8,128)(2,1)} reshape(bf16[32,197760]{1,0:T(8,128)(2,1)} %reduce.5) | data formatting | bytes 25313280 | tf_op jit(solution)/shard_map/slice | solution.py:130
  708.2 5.4 all_gather.36
  748.0 5.7 convert_bitcast_fusion
  758.2 9.5 copy.356
  767.8 40.1 %pad_maximum_fusion = bf16[6295552]{0:T(1024)(128)(2,1)} fusion(bf16[3072]{0:T(1024)(128)(2,1)S(1)} %broadcast_in_dim.66, bf16[1024]{0:T(1024)(128)(2,1)S(1)} %get-tuple-element.219, bf16[2097152]{0:T(1024)(128)(2,1)} %bitcast.230, bf16[4194304]{0:T(1024)(128)(2,1)} %bitcast.229), kind=kLoop, calls=%fused_computation.5 | loop fusion | flops 50364416 | bytes 25182208 | tf_op jit(solution)/shard_map/concatenate | solution.py:139
  807.9 11.3 convert_element_type.260
  819.2 5.5 all-to-all-start.1
  826.1 8.9 all-gather.5
  902.7 12.9 all-gather.13.cloned.1.call-done
  955.1 10.1 copy.318
  965.2 12.7 reshape.614
  978.0 5.6 fusion.116
  985.7 168.7 %concatenate.51 = bf16[6328320]{0:T(1024)(128)(2,1)} concatenate(bf16[3432448]{0:T(1024)(128)(2,1)} %reshape.614, bf16[1572864]{0:T(1024)(128)(2,1)S(1)} %bitcast.243, bf16[786432]{0:T(1024)(128)(2,1)} %reshape.616, bf16[524288]{0:T(1024)(128)(2,1)} %bitcast.247, bf16[7168]{0:T(1024)(128)(2,1)S(1)} %reshape.622, bf16[1792]{0:T(1024)(128)(2,1)S(1)} %get-tuple-element.223, ...), dimensions={0} | concatenate | bytes 25313280 | tf_op jit(solution)/shard_map/concatenate | solution.py:139
  1154.5 11.4 convert_element_type.258
  1165.8 5.5 all-to-all-start
  1171.4 30.8 %reduce_sum.317 = bf16[4,196736]{1,0:T(4,128)(2,1)} reduce(bf16[8,4,196736]{2,1,0:T(4,128)(2,1)} %all-to-all-done.1, bf16[]{:T(256)} %constant.154.clone.1), dimensions={0}, to_apply=%region_40.42 | reduce | flops 5508608 | bytes 14164994 | tf_op jit(solution)/shard_map/reduce_sum | solution.py:327
  1202.2 245.7 %all-to-all-done = bf16[8,4,197760]{2,1,0:T(4,128)(2,1)} async-done(((bf16[8,4,197760]{2,1,0:T(4,128)(2,1)}), bf16[8,4,197760]{2,1,0:T(4,128)(2,1)}, u32[]{:S(2)}, u32[]{:S(2)}) %all-to-all-start) | async-done | bytes 12656672 | tf_op jit(solution)/shard_map/all_to_all | solution.py:532
  1447.9 13.7 reduce_sum.315
  1467.8 60.9 %all-reduce.17.cloned.1.call-done = (bf16[1,4,197760]{2,1,0:T(4,128)(2,1)}, bf16[1,4,196736]{2,1,0:T(4,128)(2,1)}) async-done(((bf16[1,4,197760]{2,1,0:T(4,128)(2,1)}, bf16[1,4,196736]{2,1,0:T(4,128)(2,1)}), (bf16[1,4,197760]{2,1,0:T(4,128)(2,1)}, bf16[1,4,196736]{2,1,0:T(4,128)(2,1)})) %all-reduce.17.cloned.1.call-update) | async-done | bytes 3155984
  1528.8 9.0 multiply_subtract_fusion
  1537.8 7.3 multiply_subtract_fusion.1
  (440 shorter events, 199.8 us)
Async XLA Ops:
  7.2 161.7 %all-gather.15.cloned.1.call-start = ((), (), s32[]{:S(2)}) async-start(), calls=%async_computation.6 | async-start | bytes 26104320 | tf_op jit(solution)/shard_map/all_gather | solution.py:358
  9.7 315.0 %all-gather.17.cloned.1.call-start = ((), (), s32[]{:S(2)}) async-start(), calls=%async_computation.7 | async-start | bytes 25969152 | tf_op jit(solution)/shard_map/all_gather | solution.py:359
  11.1 707.8 %all-gather.11.cloned.1.call-start = ((), (), s32[]{:S(2)}) async-start(), calls=%async_computation.4 | async-start | bytes 3932160 | tf_op jit(solution)/shard_map/all_gather | solution.py:46
  11.1 292.5 %copy-start.90 = (f32[128]{0:T(128)}, f32[128]{0:T(128)S(1)}, u32[]{:S(2)}) copy-start(f32[128]{0:T(128)S(1)} %get-tuple-element.312) | copy-start | bytes 1540
  11.1 292.5 %copy-start.92 = (f32[128]{0:T(128)}, f32[128]{0:T(128)S(1)}, u32[]{:S(2)}) copy-start(f32[128]{0:T(128)S(1)} %get-tuple-element.313) | copy-start | bytes 1540
  11.2 292.5 %copy-start.94 = (f32[128]{0:T(128)}, f32[128]{0:T(128)S(1)}, u32[]{:S(2)}) copy-start(f32[128]{0:T(128)S(1)} %get-tuple-element.314) | copy-start | bytes 1540
  11.2 292.5 %copy-start.96 = (f32[128]{0:T(128)}, f32[128]{0:T(128)S(1)}, u32[]{:S(2)}) copy-start(f32[128]{0:T(128)S(1)} %get-tuple-element.315) | copy-start | bytes 1540
  12.9 232.8 %copy-start.117 = (f32[128]{0:T(128)}, f32[128]{0:T(128)S(1)}, u32[]{:S(2)}) copy-start(f32[128]{0:T(128)S(1)} %multiply_reduce_fusion.15) | copy-start | bytes 1540
  12.9 275.7 %copy-start.105 = (f32[128]{0:T(128)}, f32[128]{0:T(128)S(1)}, u32[]{:S(2)}) copy-start(f32[128]{0:T(128)S(1)} %fusion.144) | copy-start | bytes 1540
  13.6 288.1 %copy-start.100 = (f32[128]{0:T(128)}, f32[128]{0:T(128)S(1)}, u32[]{:S(2)}) copy-start(f32[128]{0:T(128)S(1)} %get-tuple-element.310) | copy-start | bytes 1540
  13.6 288.1 %copy-start.104 = (f32[128]{0:T(128)}, f32[128]{0:T(128)S(1)}, u32[]{:S(2)}) copy-start(f32[128]{0:T(128)S(1)} %get-tuple-element.309) | copy-start | bytes 1540
  295.9 7.8 collective-permute-start
  305.8 286.9 %copy-start.3 = (f32[128,1536]{0,1:T(8,128)}, f32[128,1536]{0,1:T(8,128)S(1)}, u32[]{:S(2)}) copy-start(f32[128,1536]{0,1:T(8,128)S(1)} %copy.282) | copy-start | bytes 2359300
  695.6 18.0 %copy-start.41 = (f32[128,512]{0,1:T(8,128)S(1)}, f32[128,512]{0,1:T(8,128)}, u32[]{:S(2)}) copy-start(f32[128,512]{0,1:T(8,128)} %copy.293) | copy-start | bytes 786436
  695.6 19.4 %copy-start.86 = (pred[128,512]{0,1:T(8,128)(4,1)S(1)}, pred[128,512]{0,1:T(8,128)(4,1)}, u32[]{:S(2)}) copy-start(pred[128,512]{0,1:T(8,128)(4,1)} %fusion.115) | copy-start | bytes 196612
  701.3 14.5 copy-start.70
  702.3 26.9 %copy-start.24 = (f32[128,1536]{1,0:T(8,128)}, f32[128,1536]{1,0:T(8,128)S(1)}, u32[]{:S(2)}) copy-start(f32[128,1536]{1,0:T(8,128)S(1)} %copy.353) | copy-start | bytes 2359300
  733.3 10.9 slice-start.1
  735.1 100.5 %copy-start.13 = (f32[128,1024]{1,0:T(8,128)}, f32[128,1024]{1,0:T(8,128)S(1)}, u32[]{:S(2)}) copy-start(f32[128,1024]{1,0:T(8,128)S(1)} %get-tuple-element.319) | copy-start | bytes 1572868
  735.1 12.8 copy-start.101
  819.2 346.6 %all-to-all-start.1 = ((bf16[8,4,196736]{2,1,0:T(4,128)(2,1)}), bf16[8,4,196736]{2,1,0:T(4,128)(2,1)}, u32[]{:S(2)}, u32[]{:S(2)}) async-start(bf16[8,4,196736]{2,1,0:T(4,128)(2,1)} %convert_element_type.260), calls=%async_computation.1 | async-start | bytes 25182208 | tf_op jit(solution)/shard_map/all_to_all | solution.py:535
  824.7 63.6 %reduce-scatter.9.cloned.1.call-start = ((), (), s32[]{:S(2)}) async-start(), calls=%async_computation.8 | async-start | bytes 163840
  851.6 42.4 %reduce-scatter.11.cloned.1.call-start = ((), (), s32[]{:S(2)}) async-start(), calls=%async_computation.9 | async-start | bytes 163840
  858.6 57.0 %all-gather.13.cloned.1.call-start = ((), (), s32[]{:S(2)}) async-start(), calls=%async_computation.5 | async-start | bytes 1966080 | tf_op jit(solution)/shard_map/all_gather | solution.py:60
  895.6 20.0 %copy-start.116 = (bf16[4,1,24]{2,0,1:T(4,128)(2,1)S(1)}, bf16[4,1,24]{2,0,1:T(4,128)(2,1)}, u32[]{:S(2)}) copy-start(bf16[4,1,24]{2,0,1:T(4,128)(2,1)} %copy.359) | copy-start | bytes 580
  944.7 4.6 collective-permute-start.1
  965.2 12.8 copy-start.36
  1165.8 282.0 %all-to-all-start = ((bf16[8,4,197760]{2,1,0:T(4,128)(2,1)}), bf16[8,4,197760]{2,1,0:T(4,128)(2,1)}, u32[]{:S(2)}, u32[]{:S(2)}) async-start(bf16[8,4,197760]{2,1,0:T(4,128)(2,1)} %convert_element_type.258), calls=%async_computation | async-start | bytes 25313280 | tf_op jit(solution)/shard_map/all_to_all | solution.py:532
  1171.3 357.4 %all-reduce.17.cloned.1.call-start = ((), (), s32[]{:S(2)}) async-start(), calls=%async_computation.10 | async-start | bytes 6311936
  1462.9 65.8 %copy-start.43 = (f32[1,197760]{1,0:T(1,128)S(1)}, f32[1,197760]{1,0:T(1,128)}, u32[]{:S(2)}) copy-start(f32[1,197760]{1,0:T(1,128)} %param.20) | copy-start | bytes 2373124
  1466.8 61.9 %copy-start.19 = (f32[1,197760]{1,0:T(1,128)S(1)}, f32[1,197760]{1,0:T(1,128)}, u32[]{:S(2)}) copy-start(f32[1,197760]{1,0:T(1,128)} %param.16) | copy-start | bytes 2373124
  1466.8 61.9 %copy-start.42 = (f32[1,197760]{1,0:T(1,128)S(1)}, f32[1,197760]{1,0:T(1,128)}, u32[]{:S(2)}) copy-start(f32[1,197760]{1,0:T(1,128)} %param.18) | copy-start | bytes 2373124
  (106 other events, 388.3 us)
Sparse Core Ops, SparseCore 0:
  11.4 157.4 all-gather.14
  172.4 152.2 all-gather.16
  326.8 26.6 all-gather.10
  851.7 20.2 reduce-scatter.8
  874.2 19.6 reduce-scatter.10
  895.9 19.6 all-gather.12
  1461.7 66.9 all-reduce.16
where the time goes:
time: 1580 us; the launch traced here: 1550 us
  waiting for transfers between devices  495 us (31%)
  other arithmetic  490 us (31%)
  local copies, waits for them, and re-layouts  413 us (26%)
  matrix products  97.4 us (6%)
  blocking collectives  25 us (2%)
  between operations  16.9 us (1%)
    all_gather x1, other arithmetic, body(): lax.all_gather(feed_params.astype(jnp.bfloat16), ('dp', 'ctx'), axis=0, t...  268 us
    all_to_all x1, waiting for transfers between devices, body(): lax.all_to_all(mixer_rows.astype(jnp.bfloat16), 'dp', split_axis=0, conca...  246 us
    concatenate x1, local copies, waits for them, and re-layouts, pack_rows(): return jnp.concatenate(members).reshape(devices, width)  169 us
    all_gather x1, waiting for transfers between devices, body(): lax.all_gather(mixer_params.astype(jnp.bfloat16), ('dp', 'ctx'), axis=0,...  155 us
    slice x6, local copies, waits for them, and re-layouts, unflatten(): result.append(flat[cursor:cursor + length].reshape(layout))  81.1 us
    all_gather x1, other arithmetic, body(): lax.all_gather(mixer_params.astype(jnp.bfloat16), ('dp', 'ctx'), axis=0,...  76.8 us
    unnamed x10, waiting for transfers between devices  65.9 us
    reduce_sum x2, other arithmetic, sources_first(): return tuple((jnp.sum(member, axis=0, keepdims=True) for member in parts))  44.5 us
  transfers between devices with their start and end apart: 11, of which 6 were waited for; matrix products, arithmetic and copies ran while one was open for 56% of the time, Pallas kernels for 0%

commit v1 on v0

v1 whole, which is shorter than its diff:
```python
import math

import jax
import jax.numpy as jnp
from jax import lax
from jax.sharding import PartitionSpec as P

D = 1024
FF = 2048
HEADS_SSM = 24
HEAD_SSM = 64
STATE = 128
KERNEL = 4
HEADS = 8
KV_HEADS = 2
HD = 64
STEP = 10
DI = 1536
CONV_COLS = 1792
QUERY_CHANNELS = 512
KEY_CHANNELS = 128
IN_COLS = 3352
QKV_COLS = 768
LANE = 128
WIDE = 1024
SMALL = KERNEL * CONV_COLS + CONV_COLS + D + 3 * HEADS_SSM

eps_norm = 1e-05
rope_base = 100000000000.0
neg_large = -1e30
beta_one = 0.9
beta_two = 0.95
learn_rate = 0.01
decay_weight = 0.1
adam_eps = 1e-08
highest = lax.Precision.HIGHEST
f32 = jnp.float32
bf16 = jnp.bfloat16


def swap(x, axis, bit):
    n = lax.axis_size(axis)
    return lax.ppermute(x, axis, [(i, i ^ bit) for i in range(n)])


def ctx_gather(x):
    n, place = lax.axis_size("ctx"), lax.axis_index("ctx")
    held, bit = x[None], n >> 1
    while bit:
        other = swap(held, "ctx", bit)
        upper = (place & bit) != 0
        low, high = jnp.where(upper, other, held), jnp.where(upper, held, other)
        held = jnp.stack([low, high], axis=1).reshape((-1,) + x.shape)
        bit >>= 1
    return held


def ctx_scatter(x):
    n, place = lax.axis_size("ctx"), lax.axis_index("ctx")
    held, bit = x, 1
    while bit < n:
        halves = held.reshape((held.shape[0] // 2, 2) + x.shape[1:])
        mine = jnp.where((place & bit) != 0, 1, 0)
        keep = lax.dynamic_index_in_dim(halves, mine, 1, False)
        send = lax.dynamic_index_in_dim(halves, 1 - mine, 1, False)
        held = keep + swap(send.astype(bf16), "ctx", bit).astype(f32)
        bit <<= 1
    return held[0]


def all_sum(x):
    for axis in ("ctx", "dp"):
        bit = 1
        while bit < lax.axis_size(axis):
            x = x + swap(x, axis, bit)
            bit <<= 1
    return x


def line_pairs(n, shift, last):
    length = n // 2
    result = []
    for z in range(length):
        to = z + shift
        far = z + last if shift > 0 else z - last
        if 0 <= to < length and 0 <= far < length:
            result += [(2 * z + y, 2 * to + y) for y in (0, 1)]
    return result


def pair_up(x, y, n, ok):
    pairs = [(i, i ^ 1) for i in range(n) if ok(i // 2)]
    other = lax.ppermute(x, "dp", pairs)
    upper = y != 0
    return jnp.stack([jnp.where(upper, other, x), jnp.where(upper, x, other)])


def dp_gather(x):
    n, place = lax.axis_size("dp"), lax.axis_index("dp")
    if n != 8:
        every = lax.all_gather(x, "dp")
        return lambda i, lo, hi: every[i, lo:hi]
    length = n // 2
    z, y = place // 2, place % 2
    right, left = x, x
    line = [pair_up(x, y, n, lambda z: True)]
    for k in range(1, length):
        right = lax.ppermute(right, "dp", [(i, i + 2) for i in range(n) if i // 2 >= k - 1 and i + 2 < n])
        left = lax.ppermute(left, "dp", [(i, i - 2) for i in range(n) if i // 2 <= length - k and i - 2 >= 0])
        line = (
            [pair_up(right, y, n, lambda z: z >= k)]
            + line
            + [pair_up(left, y, n, lambda z: z < length - k)]
        )
    line = jnp.stack(line)

    def get(i, lo, hi):
        at = length - 1 - z + i // 2
        return lax.dynamic_slice(
            line, (at, i % 2, lo, 0), (1, 1, hi - lo, x.shape[1])
        ).reshape(hi - lo, x.shape[1])

    return get


def dp_scatter(x):
    n, place = lax.axis_size("dp"), lax.axis_index("dp")
    if n != 8:
        flat = x.reshape((n * x.shape[1],) + x.shape[2:])
        return lax.psum_scatter(flat, "dp", scatter_dimension=0, tiled=True).astype(f32)
    length = n // 2
    z, y = place // 2, place % 2

    def joined(distance, ok):
        to = jnp.clip(z + distance, 0, length - 1)
        mine = lax.dynamic_index_in_dim(x, 2 * to + y, 0, False)
        theirs = lax.dynamic_index_in_dim(x, 2 * to + 1 - y, 0, False)
        pairs = [(i, i ^ 1) for i in range(n) if ok(i // 2)]
        return mine.astype(f32) + lax.ppermute(theirs, "dp", pairs).astype(f32)

    from_left = from_right = None
    for k in range(length - 1, 0, -1):
        right = joined(k, lambda z: z + k < length)
        left = joined(-k, lambda z: z - k >= 0)
        if from_left is not None:
            right, left = right + from_left, left + from_right
        from_left = lax.ppermute(
            right.astype(bf16), "dp", [(i, i + 2) for i in range(n) if i // 2 + k < length]
        ).astype(f32)
        from_right = lax.ppermute(
            left.astype(bf16), "dp", [(i, i - 2) for i in range(n) if i // 2 - k >= 0]
        ).astype(f32)
    return joined(0, lambda z: True) + from_left + from_right


def up(value, step):
    return -(-value // step) * step


class Piece:
    pass


def plan_group(mats, blocks, window, n):
    widest = LANE
    while widest < window // mats[0][2] + 32:
        widest *= 2
    plan, rows_max = [], 0
    for i in range(blocks):
        pieces, row, start = [], 0, 0
        for which, (kind, rows, width) in enumerate(mats):
            stop = start + rows * width
            lo, hi = max(start, i * window), min(stop, (i + 1) * window)
            if lo < hi:
                p = Piece()
                p.which, p.kind, p.width, p.lo, p.hi, p.start = which, kind, width, lo, hi, start
                first, last = (lo - start) // width, -(-(hi - start) // width)
                if kind == "rows":
                    p.r0, p.r1 = first // (LANE * n) * LANE * n, up(last, LANE * n)
                    spans = []
                    for c in range(n):
                        owned = [
                            r // (LANE * n) * LANE + r % LANE
                            for r in range(first, last)
                            if r // LANE % n == c
                        ]
                        if owned:
                            spans.append((owned[0], owned[-1] + 1))
                    p.t0 = min(s for s, _ in spans) // 16 * 16
                    p.t1 = up(max(e for _, e in spans), 16)
                    p.count = p.t1 - p.t0
                elif kind == "qkv":
                    p.r0, p.r1 = first // 64 * 64, up(last, 64)
                    p.count = (p.r1 - p.r0) // 4
                else:
                    p.r0, p.r1 = first // 16 * 16, up(last, 16)
                    p.count = p.r1 - p.r0
                p.row = row
                row += p.count
                if kind == "in":
                    p.lanes = widest
                    p.extra = row
                    row += up(HEADS_SSM * widest // WIDE, 16)
                pieces.append(p)
            start = stop
        plan.append(pieces)
        rows_max = max(rows_max, row)
    return plan, rows_max


def mixer_mats():
    return [
        ("in", D, IN_COLS),
        ("rows", DI, D),
        ("qkv", D, QKV_COLS),
        ("rows", QUERY_CHANNELS, D),
        ("same", up(SMALL, WIDE) // WIDE, WIDE),
    ]


def feed_mats():
    return [("up", D, 2 * FF), ("rows", FF, D), ("same", 1, D)]


def own_blocks(x, first, count, n, place):
    result = []
    for j in range(count // n):
        at = first + j * n * LANE
        block = x[:, at : at + LANE]
        for c in range(1, n):
            block = jnp.where(place == c, x[:, at + c * LANE : at + (c + 1) * LANE], block)
        result.append(block)
    return result


def all_blocks(x, first, count, n, place):
    result = []
    for b in range(count):
        block = x[:, first + b // n * LANE : first + (b // n + 1) * LANE]
        result.append(jnp.where(place == b % n, block, jnp.zeros_like(block)))
    return result


def pick_message(pieces, rows_max, window, index, n, flat, place):
    parts, filled = [], 0
    for p in pieces:
        cut = flat[p.lo - index * window : p.hi - index * window]
        front = p.lo - p.start - p.r0 * p.width
        back = (p.r1 - p.r0) * p.width - front - (p.hi - p.lo)
        x = jnp.pad(cut, (front, back)).reshape(p.r1 - p.r0, p.width)
        rows = x.shape[0]
        if p.kind == "in":
            blocks = own_blocks(x, 0, DI // LANE, n, place) + own_blocks(x, DI, DI // LANE, n, place)
            blocks.append(x[:, 2 * DI : DI + CONV_COLS])
            parts.append(jnp.concatenate(blocks, axis=1))
            groups = WIDE // p.lanes
            each = HEADS_SSM // groups
            steps = jnp.pad(x[:, DI + CONV_COLS :].T, ((0, 0), (0, p.lanes - rows)))
            steps = jnp.concatenate([steps[g * each : (g + 1) * each] for g in range(groups)], axis=1)
            parts.append(jnp.pad(steps, ((0, up(each, 16) - each), (0, 0))))
        elif p.kind == "up":
            blocks = own_blocks(x, 0, FF // LANE, n, place) + own_blocks(x, FF, FF // LANE, n, place)
            parts.append(jnp.concatenate(blocks, axis=1))
        elif p.kind == "rows":
            x = x.reshape(rows // (LANE * n), n, LANE, WIDE)
            x = lax.dynamic_index_in_dim(x, place, 1, False).reshape(rows // n, WIDE)
            base = p.r0 // n
            parts.append(x[p.t0 - base : p.t1 - base])
        elif p.kind == "qkv":
            per = QUERY_CHANNELS // n
            half = place * KV_HEADS // n
            q = x[:, :per]
            for c in range(1, n):
                q = jnp.where(place == c, x[:, c * per : (c + 1) * per], q)
            kv = []
            for first in (QUERY_CHANNELS, QUERY_CHANNELS + KEY_CHANNELS):
                kv.append(
                    jnp.where(half == 0, x[:, first : first + HD], x[:, first + HD : first + 2 * HD])
                )
            x = jnp.concatenate([q] + kv, axis=1)
            parts.append(
                jnp.concatenate([x[g * p.count : (g + 1) * p.count] for g in range(4)], axis=1)
            )
        else:
            parts.append(x)
        filled = p.row + p.count
        if p.kind == "in":
            filled = p.extra + up(HEADS_SSM * p.lanes // WIDE, 16)
    if filled < rows_max:
        parts.append(jnp.zeros((rows_max - filled, WIDE), flat.dtype))
    return jnp.concatenate(parts, axis=0)


def join_message(plan, which, rows, get):
    total = None
    for i, pieces in enumerate(plan):
        for p in pieces:
            if p.which != which:
                continue
            x = get(i, p.row, p.row + p.count)
            first = p.r0
            if p.kind == "rows":
                first = p.t0
            if p.kind == "qkv":
                x = jnp.concatenate([x[:, g * 256 : (g + 1) * 256] for g in range(4)], axis=0)
            x = x[: rows - first]
            x = jnp.pad(x, ((first, rows - first - x.shape[0]), (0, 0)))
            total = x if total is None else total + x
    return total


def join_steps(plan, get):
    total = None
    for i, pieces in enumerate(plan):
        for p in pieces:
            if p.kind != "in":
                continue
            groups = WIDE // p.lanes
            each = HEADS_SSM // groups
            x = get(i, p.extra, p.extra + up(each, 16))[:each]
            x = jnp.concatenate([x[:, g * p.lanes : (g + 1) * p.lanes] for g in range(groups)], axis=0)
            count = min(p.r1, D) - p.r0
            x = jnp.pad(x[:, :count], ((0, 0), (p.r0, D - p.r0 - count)))
            total = x if total is None else total + x
    return total


def fill_message(pieces, rows_max, grads, steps):
    parts, filled = [], 0

    def rows_of(x, lo, hi):
        have = x[lo : min(hi, x.shape[0])]
        return jnp.pad(have, ((0, hi - lo - have.shape[0]), (0, 0)))

    for p in pieces:
        x = grads[p.which]
        if p.kind == "rows":
            parts.append(rows_of(x, p.t0, p.t1))
        elif p.kind == "qkv":
            parts.append(
                jnp.concatenate(
                    [rows_of(x, p.r0 + g * p.count, p.r0 + (g + 1) * p.count) for g in range(4)], axis=1
                )
            )
        else:
            parts.append(rows_of(x, p.r0, p.r1))
        filled = p.row + p.count
        if p.kind == "in":
            groups = WIDE // p.lanes
            each = HEADS_SSM // groups
            count = min(p.r1, D) - p.r0
            part = jnp.pad(steps[:, p.r0 : p.r0 + count], ((0, 0), (0, p.lanes - count)))
            part = jnp.concatenate([part[g * each : (g + 1) * each] for g in range(groups)], axis=1)
            parts.append(jnp.pad(part, ((0, up(each, 16) - each), (0, 0))))
            filled = p.extra + up(each, 16)
    if filled < rows_max:
        parts.append(jnp.zeros((rows_max - filled, WIDE), bf16))
    return jnp.concatenate(parts, axis=0)


def spread_message(pieces, window, index, n, message, extra_one, place):
    parts, filled = [], 0
    for p in pieces:
        x = message[p.row : p.row + p.count]
        rows = p.r1 - p.r0
        if p.kind == "in":
            groups = WIDE // p.lanes
            each = HEADS_SSM // groups
            steps = message[p.extra : p.extra + each]
            steps = jnp.concatenate(
                [steps[:, g * p.lanes : (g + 1) * p.lanes] for g in range(groups)], axis=0
            )
            steps = steps[:, :rows].T
            own = DI // n
            blocks = all_blocks(x, 0, DI // LANE, n, place) + all_blocks(x, own, DI // LANE, n, place)
            x = jnp.concatenate(blocks + [x[:, 2 * own : 2 * own + 2 * STATE], steps], axis=1)
        elif p.kind == "up":
            own = FF // n
            blocks = all_blocks(x, 0, FF // LANE, n, place) + all_blocks(x, own, FF // LANE, n, place)
            x = jnp.concatenate(blocks, axis=1)
        elif p.kind == "rows":
            base = p.r0 // n
            x = jnp.pad(x, ((p.t0 - base, p.r1 // n - p.t1), (0, 0)))
            x = x.reshape(rows // (LANE * n), 1, LANE, WIDE)
            at = jnp.arange(n, dtype=jnp.int32)[None, :, None, None] == place
            x = jnp.where(at, x, jnp.zeros((), x.dtype)).reshape(rows, WIDE)
        elif p.kind == "qkv":
            x = jnp.concatenate([x[:, g * 256 : (g + 1) * 256] for g in range(4)], axis=0)
            per = QUERY_CHANNELS // n
            half = place * KV_HEADS // n
            zero = jnp.zeros((), x.dtype)
            blocks = [jnp.where(place == c, x[:, :per], zero) for c in range(n)]
            for first in (per, per + HD):
                blocks += [jnp.where(half == h, x[:, first : first + HD], zero) for h in range(KV_HEADS)]
            x = jnp.concatenate(blocks, axis=1)
        elif extra_one is not None:
            x = x[: extra_one.shape[0] + p.r0][: p.r1 - p.r0]
            more = extra_one[p.r0 : p.r1]
            more = jnp.pad(more, ((0, x.shape[0] - more.shape[0]), (0, 0)))
            x = x + jnp.where(place == 0, more, jnp.zeros((), x.dtype))
        front = p.lo - p.start - p.r0 * p.width
        parts.append(x.reshape(-1)[front : front + p.hi - p.lo])
        filled = p.hi - index * window
    if filled < window:
        parts.append(jnp.zeros((window - filled,), message.dtype))
    return jnp.concatenate(parts) if len(parts) > 1 else parts[0]


def distribute(shard, plan, rows_max, n):
    place, at = lax.axis_index("ctx"), lax.axis_index("dp")
    width = shard.shape[1]
    window = n * width
    flat = ctx_gather(shard.astype(bf16).reshape(width // LANE, LANE)).reshape(-1)
    branches = [
        (lambda flat, place, i=i: pick_message(plan[i], rows_max, window, i, n, flat, place))
        for i in range(len(plan))
    ]
    return dp_gather(lax.switch(at, branches, flat, place))


def collect(plan, rows_max, n, width, grads, steps, extra_one=None):
    place, at = lax.axis_index("ctx"), lax.axis_index("dp")
    window = n * width
    rows = jnp.stack([fill_message(pieces, rows_max, grads, steps) for pieces in plan])
    message = dp_scatter(rows)
    if extra_one is None:
        branches = [
            (lambda m, place, i=i: spread_message(plan[i], window, i, n, m, None, place))
            for i in range(len(plan))
        ]
        flat = lax.switch(at, branches, message, place)
    else:
        branches = [
            (lambda m, e, place, i=i: spread_message(plan[i], window, i, n, m, e, place))
            for i in range(len(plan))
        ]
        flat = lax.switch(at, branches, message, extra_one, place)
    return ctx_scatter(flat.reshape(n, width // LANE, LANE)).reshape(1, width)


def rms_scale(values):
    return lax.rsqrt(jnp.mean(values * values, axis=-1, keepdims=True) + eps_norm)


def rms_back(values, gain, grad):
    scale = rms_scale(values)
    unit = values * scale
    inner = grad * gain
    grad_values = scale * (inner - unit * jnp.mean(inner * unit, axis=-1, keepdims=True))
    return grad_values, jnp.sum(grad * unit, axis=0)


def swiglu(gate_up):
    half = gate_up.shape[1] // 2
    return jax.nn.silu(gate_up[:, :half]) * gate_up[:, half:]


def gate_product(ssm_out, ssm_gate):
    return ssm_out * jax.nn.silu(ssm_gate)


def causal_conv(positions, conv_input, conv_weight, conv_bias):
    row_count = positions.shape[0]
    extended = jnp.pad(conv_input, ((KERNEL - 1, 0), (0, 0)))
    summed = jnp.broadcast_to(conv_bias[None, :], conv_input.shape)
    for tap_index in range(KERNEL):
        first_row = KERNEL - 1 - tap_index
        earlier = extended[first_row : first_row + row_count]
        usable = (positions >= tap_index).astype(f32)[:, None]
        summed = summed + usable * earlier * conv_weight[tap_index][None, :]
    return jax.nn.silu(summed)


def rope_tables(positions):
    half_dim = HD // 2
    frequency = jnp.exp(-jnp.log(rope_base) * jnp.arange(half_dim, dtype=f32) * 2.0 / HD)
    angles = positions.astype(f32)[:, None] * frequency[None, :]
    return (jnp.cos(angles), jnp.sin(angles))


def apply_rotary(values, cosine_table, sine_table, reverse):
    row_count = values.shape[0]
    half_dim = HD // 2
    per_head = values.reshape(row_count, -1, HD)
    first_half = per_head[..., :half_dim]
    second_half = per_head[..., half_dim:]
    cos_wide = cosine_table[:, None, :]
    sin_wide = sine_table[:, None, :]
    if reverse:
        sin_wide = -sin_wide
    rotated = jnp.concatenate(
        [
            first_half * cos_wide - second_half * sin_wide,
            second_half * cos_wide + first_half * sin_wide,
        ],
        axis=-1,
    )
    return rotated.reshape(row_count, -1)


def attention_mask(positions):
    index = jnp.arange(positions.shape[0], dtype=jnp.int32)
    return (index[None, :] <= index[:, None]) & (index[None, :] >= (index - positions)[:, None])


def attend(queries, keys, values, allowed):
    row_count = queries.shape[0]
    heads = queries.reshape(row_count, -1, HD)
    scores = jnp.einsum("rhd,sd->hrs", heads, keys, preferred_element_type=f32) * HD ** (-0.5)
    unnormed = jnp.exp(jnp.where(allowed[None], scores, neg_large))
    row_sum = jnp.sum(unnormed, axis=-1, keepdims=True)
    mixed = (
        jnp.einsum("hrs,sd->hrd", unnormed.astype(bf16), values, preferred_element_type=f32) / row_sum
    )
    attended = jnp.transpose(mixed, (1, 0, 2)).reshape(row_count, -1)
    return attended, jnp.log(row_sum[..., 0])


def attend_back(queries, keys, values, attended_b, grad_att_b, log_total, allowed):
    row_count = queries.shape[0]
    heads = queries.reshape(row_count, -1, HD)
    scores = jnp.einsum("rhd,sd->hrs", heads, keys, preferred_element_type=f32) * HD ** (-0.5)
    probs = jnp.exp(jnp.where(allowed[None], scores - log_total[..., None], neg_large))
    gradient_heads = grad_att_b.reshape(row_count, -1, HD)
    out_heads = attended_b.reshape(row_count, -1, HD)
    grad_probs = jnp.einsum("rhd,sd->hrs", gradient_heads, values, preferred_element_type=f32)
    row_dot = jnp.sum(gradient_heads.astype(f32) * out_heads.astype(f32), axis=-1).T
    gradient_scores = (probs * (grad_probs - row_dot[..., None]) * HD ** (-0.5)).astype(bf16)
    grad_queries = jnp.einsum("hrs,sd->rhd", gradient_scores, keys, preferred_element_type=f32)
    gradient_keys = jnp.einsum("hrs,rhd->sd", gradient_scores, heads, preferred_element_type=f32)
    gradient_values = jnp.einsum(
        "hrs,rhd->sd", probs.astype(bf16), gradient_heads, preferred_element_type=f32
    )
    return grad_queries.reshape(row_count, -1), gradient_keys, gradient_values


def ssm(allowed, ssm_input, state_write, state_read, step_raw, bias_step, log_rate, skip_gain):
    row_count = ssm_input.shape[0]
    step_size = jax.nn.softplus(step_raw + bias_step[None, :])
    log_step = -jnp.exp(log_rate)[None, :] * step_size
    index = jnp.arange(row_count, dtype=jnp.int32)
    below = (index[None, :] <= index[:, None]).astype(f32)
    cumulative = jnp.dot(below, log_step, precision=highest)
    x = ssm_input.reshape(row_count, -1, HEAD_SSM)
    weighted = x * step_size[:, :, None]
    gaps = cumulative.T[:, :, None] - cumulative.T[:, None, :]
    decay = jnp.exp(jnp.where(allowed[None], gaps, neg_large))
    read_write = jnp.dot(state_read, state_write.T, precision=highest)
    out = jnp.einsum("hts,shp->thp", read_write[None] * decay, weighted, precision=highest)
    return (out + skip_gain[None, :, None] * x).reshape(row_count, -1)


def adam_step(weights, grads, first_state, second_state):
    first_next = beta_one * first_state + (1.0 - beta_one) * grads
    second_next = beta_two * second_state + (1.0 - beta_two) * grads * grads
    first_hat = first_next / (1.0 - beta_one**STEP)
    second_hat = second_next / (1.0 - beta_two**STEP)
    weight_next = weights - learn_rate * (
        first_hat / (jnp.sqrt(second_hat) + adam_eps) + decay_weight * weights
    )
    return (weight_next, first_next, second_next)


def dot(a, b):
    return jnp.dot(a, b, preferred_element_type=f32)


def dot_t(a, b):
    return lax.dot_general(a, b, (((1,), (1,)), ((), ())), preferred_element_type=f32)


def t_dot(a, b):
    return lax.dot_general(a, b, (((0,), (0,)), ((), ())), preferred_element_type=f32)


def body(
    hidden_in,
    positions,
    mixer_params,
    feed_params,
    mixer_first,
    feed_first,
    mixer_second,
    feed_second,
    out_grad,
):
    n, blocks = lax.axis_size("ctx"), lax.axis_size("dp")
    place = lax.axis_index("ctx")
    mixer_width, feed_width = mixer_params.shape[1], feed_params.shape[1]
    mixer_plan, mixer_rows = plan_group(mixer_mats(), blocks, n * mixer_width, n)
    feed_plan, feed_rows = plan_group(feed_mats(), blocks, n * feed_width, n)
    row_count = hidden_in.shape[0]

    get_mixer = distribute(mixer_params, mixer_plan, mixer_rows, n)
    positions = ctx_gather(positions[None])[:, 0].reshape(-1)
    out_grad_b = ctx_gather(out_grad.astype(bf16)).reshape(-1, D)

    own_di, own_q = DI // n, QUERY_CHANNELS // n
    w_in = join_message(mixer_plan, 0, D, get_mixer)
    w_ssm_out = join_message(mixer_plan, 1, DI // n, get_mixer)
    w_qkv = join_message(mixer_plan, 2, D, get_mixer)
    w_attn_out = join_message(mixer_plan, 3, own_q, get_mixer)
    small = join_message(mixer_plan, 4, up(SMALL, WIDE) // WIDE, get_mixer).reshape(-1).astype(f32)
    w_step = join_steps(mixer_plan, get_mixer)
    get_feed = distribute(feed_params, feed_plan, feed_rows, n)
    w_gate_up = join_message(feed_plan, 0, D, get_feed)
    w_down = join_message(feed_plan, 1, FF // n, get_feed)
    gain_two = join_message(feed_plan, 2, 1, get_feed).reshape(D).astype(f32)
    w_mix_out = jnp.concatenate([w_ssm_out, w_attn_out], axis=0)

    pairs = HEADS_SSM // (2 * n)

    def own_heads(x, axis):
        shape = x.shape[:axis] + (pairs, n, 2) + x.shape[axis + 1 :]
        picked = lax.dynamic_index_in_dim(x.reshape(shape), place, axis + 1, False)
        return picked.reshape(x.shape[:axis] + (2 * pairs,) + x.shape[axis + 1 :])

    def all_heads(x, axis):
        shape = x.shape[:axis] + (pairs, 1, 2) + x.shape[axis + 1 :]
        at = jnp.arange(n, dtype=jnp.int32) == place
        at = at.reshape((1,) * (axis + 1) + (n, 1) + (1,) * (x.ndim - axis - 1))
        spread = jnp.where(at, x.reshape(shape), jnp.zeros((), x.dtype))
        return spread.reshape(x.shape[:axis] + (HEADS_SSM,) + x.shape[axis + 1 :])

    def own_conv(x):
        parts = own_blocks(x, 0, DI // LANE, n, place)
        return jnp.concatenate(parts + [x[:, DI:]], axis=1)

    def all_conv(x):
        parts = all_blocks(x, 0, DI // LANE, n, place)
        return jnp.concatenate(parts + [x[:, own_di:]], axis=1)

    cut = KERNEL * CONV_COLS
    conv_weight = own_conv(small[:cut].reshape(KERNEL, CONV_COLS))
    conv_bias = own_conv(small[cut : cut + CONV_COLS].reshape(1, CONV_COLS))[0]
    cut += CONV_COLS
    gain_one = small[cut : cut + D]
    cut += D
    bias_step = own_heads(small[cut : cut + HEADS_SSM], 0)
    log_rate = own_heads(small[cut + HEADS_SSM : cut + 2 * HEADS_SSM], 0)
    skip_gain = own_heads(small[cut + 2 * HEADS_SSM : cut + 3 * HEADS_SSM], 0)
    w_step_own = own_heads(w_step, 0)

    normed_own = (hidden_in * rms_scale(hidden_in) * gain_one).astype(bf16)
    normed_b = ctx_gather(normed_own).reshape(-1, D)
    projected = dot(normed_b, w_in)
    step_raw = dot_t(normed_b, w_step_own)
    query_key_value = dot(normed_b, w_qkv)
    ssm_gate = projected[:, :own_di]
    conv_input = projected[:, own_di:]
    allowed = attention_mask(positions)
    conv_out, conv_back = jax.vjp(
        lambda a, w, b: causal_conv(positions, a, w, b), conv_input, conv_weight, conv_bias
    )
    ssm_out, ssm_back = jax.vjp(
        lambda *args: ssm(allowed, *args),
        conv_out[:, :own_di],
        conv_out[:, own_di : own_di + STATE],
        conv_out[:, own_di + STATE :],
        step_raw,
        bias_step,
        log_rate,
        skip_gain,
    )
    gated, gate_back = jax.vjp(gate_product, ssm_out, ssm_gate)
    cosine_table, sine_table = rope_tables(positions)
    queries = apply_rotary(query_key_value[:, :own_q], cosine_table, sine_table, False).astype(bf16)
    keys = apply_rotary(
        query_key_value[:, own_q : own_q + HD], cosine_table, sine_table, False
    ).astype(bf16)
    values = query_key_value[:, own_q + HD :].astype(bf16)
    attended, log_total = attend(queries, keys, values, allowed)
    mixed_b = jnp.concatenate([gated.astype(bf16), attended.astype(bf16)], axis=1)
    branches = ctx_scatter(dot(mixed_b, w_mix_out).reshape(n, row_count, D))
    residual = hidden_in + branches

    normed_two_own = (residual * rms_scale(residual) * gain_two).astype(bf16)
    normed_two_b = ctx_gather(normed_two_own).reshape(-1, D)
    gate_up = dot(normed_two_b, w_gate_up)
    activated, swiglu_back = jax.vjp(swiglu, gate_up)
    activated_b = activated.astype(bf16)
    block_out = residual + ctx_scatter(dot(activated_b, w_down).reshape(n, row_count, D))

    grad_w_down = t_dot(activated_b, out_grad_b).astype(bf16)
    grad_activated = dot_t(out_grad_b, w_down)
    grad_gate_up = swiglu_back(grad_activated)[0].astype(bf16)
    grad_normed_two = ctx_scatter(dot_t(grad_gate_up, w_gate_up).reshape(n, row_count, D))
    grad_w_gate_up = t_dot(normed_two_b, grad_gate_up).astype(bf16)
    grad_resid_mlp, grad_gain_two = rms_back(residual, gain_two, grad_normed_two)
    grad_residual = out_grad + grad_resid_mlp
    feed_grad = collect(
        feed_plan,
        feed_rows,
        n,
        feed_width,
        (grad_w_gate_up, grad_w_down, grad_gain_two.astype(bf16)[None]),
        None,
    )

    grad_mix_b = ctx_gather(grad_residual.astype(bf16)).reshape(-1, D)
    grad_mixed = dot_t(grad_mix_b, w_mix_out)
    grad_w_mix_out = t_dot(mixed_b, grad_mix_b).astype(bf16)
    grad_ssm_out, grad_ssm_gate = gate_back(grad_mixed[:, :own_di])
    grad_in, grad_write, grad_read, grad_step, grad_bias, grad_rate, grad_skip = ssm_back(grad_ssm_out)
    grad_conv_input, grad_conv_weight, grad_conv_bias = conv_back(
        jnp.concatenate([grad_in, grad_write, grad_read], axis=1)
    )
    grad_projected = jnp.concatenate([grad_ssm_gate, grad_conv_input], axis=1).astype(bf16)
    grad_step_b = grad_step.astype(bf16)
    grad_att_b = grad_mixed[:, own_di:].astype(bf16)
    grad_queries, grad_keys, grad_values = attend_back(
        queries, keys, values, mixed_b[:, own_di:], grad_att_b, log_total, allowed
    )
    grad_qkv = jnp.concatenate(
        [
            apply_rotary(grad_queries, cosine_table, sine_table, True),
            apply_rotary(grad_keys, cosine_table, sine_table, True),
            grad_values,
        ],
        axis=1,
    ).astype(bf16)
    partial_one = (
        dot_t(grad_projected, w_in) + dot_t(grad_qkv, w_qkv) + dot(grad_step_b, w_step_own)
    )
    grad_normed_one = ctx_scatter(partial_one.reshape(n, row_count, D))
    grad_w_in = t_dot(normed_b, grad_projected).astype(bf16)
    grad_w_qkv = t_dot(normed_b, grad_qkv).astype(bf16)
    grad_w_step = all_heads(t_dot(grad_step_b, normed_b).astype(bf16), 0)
    grad_resid_norm, grad_gain_one = rms_back(hidden_in, gain_one, grad_normed_one)
    grad_input = grad_residual + grad_resid_norm
    gain_sum = all_sum(grad_gain_one.reshape(D // LANE, LANE)).reshape(-1)
    before, after = KERNEL * CONV_COLS + CONV_COLS, 3 * HEADS_SSM
    small_size = up(SMALL, WIDE)
    gain_rows = jnp.pad(gain_sum, (before, small_size - before - D)).reshape(-1, WIDE)
    small_grads = jnp.concatenate(
        [
            all_conv(grad_conv_weight).reshape(-1),
            all_conv(grad_conv_bias[None])[0],
            jnp.zeros((D,), f32),
            all_heads(grad_bias, 0),
            all_heads(grad_rate, 0),
            all_heads(grad_skip, 0),
            jnp.zeros((small_size - SMALL,), f32),
        ]
    ).reshape(-1, WIDE)
    mixer_grad = collect(
        mixer_plan,
        mixer_rows,
        n,
        mixer_width,
        (
            grad_w_in,
            grad_w_mix_out[:own_di],
            grad_w_qkv,
            grad_w_mix_out[own_di:],
            small_grads.astype(bf16),
        ),
        grad_w_step,
        gain_rows,
    )

    mixer_new, mixer_first_new, mixer_second_new = adam_step(
        mixer_params, mixer_grad, mixer_first, mixer_second
    )
    feed_new, feed_first_new, feed_second_new = adam_step(
        feed_params, feed_grad, feed_first, feed_second
    )
    return (
        block_out,
        grad_input,
        mixer_grad,
        feed_grad,
        mixer_new,
        feed_new,
        mixer_first_new,
        feed_first_new,
        mixer_second_new,
        feed_second_new,
    )


def solution(mesh):
    in_specs = (
        P(("dp", "ctx"), None),
        P(("dp", "ctx")),
        P(("dp", "ctx"), None),
        P(("dp", "ctx"), None),
        P(("dp", "ctx"), None),
        P(("dp", "ctx"), None),
        P(("dp", "ctx"), None),
        P(("dp", "ctx"), None),
        P(("dp", "ctx"), None),
    )
    out_specs = (
        P(("dp", "ctx"), None),
        P(("dp", "ctx"), None),
        P(("dp", "ctx"), None),
        P(("dp", "ctx"), None),
        P(("dp", "ctx"), None),
        P(("dp", "ctx"), None),
        P(("dp", "ctx"), None),
        P(("dp", "ctx"), None),
        P(("dp", "ctx"), None),
        P(("dp", "ctx"), None),
    )
    return jax.shard_map(body, mesh=mesh, in_specs=in_specs, out_specs=out_specs, check_vma=False)
```

time: 1580 us -> 693 us (0.44)
  other arithmetic: 490 us -> 150 us
  waiting for transfers between devices: 495 us -> 162 us
  local copies, waits for them, and re-layouts: 413 us -> 140 us
  starting transfers between devices: 14.9 us -> 134 us
  matrix products: 97.4 us -> 60.7 us
  loops' own time: 0.53 us -> 27.6 us
  blocking collectives: 25 us -> 0 us
    all_gather x2 -> x0, other arithmetic: 345 us -> none  [the longest x1 268 us: body(): lax.all_gather(feed_params.astype(jnp.bfloat16), ('dp', 'ctx'), axis=0, t...]
    all_to_all x2 -> x0, waiting for transfers between devices: 246 us -> none  [the longest x1 246 us: body(): lax.all_to_all(mixer_rows.astype(jnp.bfloat16), 'dp', split_axis=0, conca...]
    all_gather x4 -> x0, waiting for transfers between devices: 183 us -> none  [the longest x1 155 us: body(): lax.all_gather(mixer_params.astype(jnp.bfloat16), ('dp', 'ctx'), axis=0,...]
    concatenate x1 -> x9, local copies, waits for them, and re-layouts: 169 us -> 3.8 us  [the longest x2 1.21 us: fill_message(): return jnp.concatenate(parts, axis=0)]
    ppermute x2 -> x83, waiting for transfers between devices: 0.01 us -> 162 us  [the longest x6 40.9 us: dp_gather(): lax.ppermute(left, 'dp', [(i, i - 2) for i in range(n) if i // 2 <= lengt...]
    ppermute x2 -> x83, starting transfers between devices: 3.44 us -> 134 us  [the longest x31 33.6 us: swap(): return lax.ppermute(x, axis, [(i, i ^ bit) for i in range(n)])]
    slice x22 -> x48, local copies, waits for them, and re-layouts: 85.4 us -> 15.3 us  [the longest x2 3.21 us: body(): conv_out[:, :own_di]]
    unnamed x10 -> x0, waiting for transfers between devices: 65.9 us -> none
  transfers between devices with their start and end apart: 11 -> 83, of which waited for: 6 -> 30; matrix products, arithmetic and copies ran while one was open for 56% -> 46% of each run, Pallas kernels for 0% -> 0%
where the time goes in v1:
time: 693 us; the launch traced here: 680 us
  waiting for transfers between devices  162 us (23%)
  other arithmetic  150 us (22%)
  local copies, waits for them, and re-layouts  140 us (20%)
  starting transfers between devices  134 us (19%)
  matrix products  60.7 us (9%)
  loops' own time  27.6 us (4%)
    ppermute x6, waiting for transfers between devices, dp_gather(): lax.ppermute(left, 'dp', [(i, i - 2) for i in range(n) if i // 2 <= lengt...  40.9 us
    ppermute x14, waiting for transfers between devices, pair_up(): other = lax.ppermute(x, 'dp', pairs)  37.6 us
    ppermute x31, waiting for transfers between devices, swap(): return lax.ppermute(x, axis, [(i, i ^ bit) for i in range(n)])  36.6 us
    ppermute x14, waiting for transfers between devices, joined(): return mine.astype(f32) + lax.ppermute(theirs, 'dp', pairs).astype(f32)  36 us
    ppermute x31, starting transfers between devices, swap(): return lax.ppermute(x, axis, [(i, i ^ bit) for i in range(n)])  33.6 us
    unnamed x308, local copies, waits for them, and re-layouts  32 us
    cond x68, other arithmetic  29.5 us
    dot_general x3, matrix products, ssm(): jnp.einsum('hts,shp->thp', read_write[None] * decay, weighted, precision=...  27 us
  transfers between devices with their start and end apart: 83, of which 30 were waited for; matrix products, arithmetic and copies ran while one was open for 46% of the time, Pallas kernels for 0%

profile of v1, /device:TPU:0, one launch (start us, length us, event | category | flops | bytes accessed | tf_op | source)
XLA Modules:
  0.0 679.7 jit_solution(17527121524854160834)
XLA Ops:
  5.6 9.2 %convert_reduce_fusion.1 = bf16[196736]{0:T(1024)(128)(2,1)S(1)} fusion(f32[1,196736]{1,0:T(1,128)} %param.44), kind=kLoop, calls=%fused_computation.995 | loop fusion | flops 196736 | bytes 1180416 | tf_op jit(solution)/shard_map/convert_element_type | solution.py:413
  16.7 8.2 %convert_reduce_fusion = bf16[197760]{0:T(1024)(128)(2,1)S(1)} fusion(f32[1,197760]{1,0:T(1,128)S(1)} %copy-done.15), kind=kLoop, calls=%fused_computation.983 | loop fusion | flops 197760 | bytes 1186560 | tf_op jit(solution)/shard_map/convert_element_type | solution.py:413
  31.1 6.6 copy.338
  40.6 6.5 copy.324
  52.0 13.7 %conditional.5 = (bf16[272,1024]{1,0:T(8,128)(2,1)}) conditional(s32[]{:T(128)} %clamp.2, (s32[]{:T(128)}, bf16[786944]{0:T(1024)(128)(2,1)S(1)}) %tuple.148, (s32[]{:T(128)}, bf16[786944]{0:T(1024)(128)(2,1)S(1)}) %tuple.148, (s32[]{:T(128)}, bf16[786944]{0:T(1024)(128)(2,1)S(1)}) %tuple.148, (s32[]{:T(128)}, ...), branch_computations={%region_11.12_spmd, %region_12.13_spmd, %region_13.14_spmd, %regio... | conditional | flops 1867781 | bytes 15864233 | solution.py:418
  79.3 22.9 %conditional.4 = (bf16[304,1024]{1,0:T(8,128)(2,1)S(1)}) conditional(s32[]{:T(128)} %clamp.2, (s32[]{:T(128)}, bf16[791040]{0:T(1024)(128)(2,1)S(1)}) %tuple.146, (s32[]{:T(128)}, bf16[791040]{0:T(1024)(128)(2,1)S(1)}) %tuple.146, (s32[]{:T(128)}, bf16[791040]{0:T(1024)(128)(2,1)S(1)}) %tuple.146, (s32[]{:T(128)}, ...), branch_computations={%region_0.1_spmd, %region_1.2_spmd, %region_2.3_spmd, %region_3.4_... | conditional | flops 5144599 | bytes 15789308 | solution.py:418
  125.1 6.2 collective-permute-done.32
  140.2 5.6 collective-permute-done.10
  161.7 7.7 %collective-permute-done.12 = bf16[304,1024]{1,0:T(8,128)(2,1)S(1)} collective-permute-done((bf16[304,1024]{1,0:T(8,128)(2,1)S(1)}, bf16[304,1024]{1,0:T(8,128)(2,1)S(1)}, u32[]{:S(2)}, u32[]{:S(2)}) %collective-permute-start.12) | collective-permute-done | bytes 622624 | tf_op jit(solution)/shard_map/ppermute | solution.py:93
  170.2 30.2 %collective-permute-done.34 = bf16[272,1024]{1,0:T(8,128)(2,1)} collective-permute-done((bf16[272,1024]{1,0:T(8,128)(2,1)S(1)}, bf16[272,1024]{1,0:T(8,128)(2,1)}, u32[]{:S(2)}, u32[]{:S(2)}) %collective-permute-start.34) | collective-permute-done | bytes 557088 | tf_op jit(solution)/shard_map/ppermute | solution.py:109
  211.0 19.8 %collective-permute-done.14 = bf16[304,1024]{1,0:T(8,128)(2,1)S(1)} collective-permute-done((bf16[304,1024]{1,0:T(8,128)(2,1)S(1)}, bf16[304,1024]{1,0:T(8,128)(2,1)S(1)}, u32[]{:S(2)}, u32[]{:S(2)}) %collective-permute-start.14) | collective-permute-done | bytes 622624 | tf_op jit(solution)/shard_map/ppermute | solution.py:93
  278.8 9.6 %fusion.300 = f32[512,6,64]{0,2,1:T(8,128)} fusion(f32[6,512]{1,0:T(8,128)S(1)} %fusion.363, f32[512,512]{1,0:T(8,128)} %fusion.420, pred[512,512]{1,0:T(8,128)(4,1)} %copy.331, f32[512,6,64]{0,2,1:T(8,128)} %bitcast.739, f32[6]{0:T(128)S(1)} %copy-done.142, f32[512,6]{0,1:T(8,128)S(1)} %get-tuple-element.786), kind=kOutput, calls=%fused_computation.849 | convolution fusion | flops 1213267968 | bytes 2908184 | tf_op jit(solution)/shard_map/jvp(hts,shp->thp)/dot_general | solution.py:549
  331.8 6.9 %collective-permute-done.43 = bf16[1,128,1024]{2,1,0:T(8,128)(2,1)S(1)} collective-permute-done((bf16[1,128,1024]{2,1,0:T(8,128)(2,1)S(1)}, bf16[1,128,1024]{2,1,0:T(8,128)(2,1)S(1)}, u32[]{:S(2)}, u32[]{:S(2)}) %collective-permute-start.43) | collective-permute-done | bytes 262176 | tf_op jit(solution)/shard_map/ppermute | solution.py:43
  346.2 6.2 collective-permute-done.44
  377.7 11.3 %fusion.270 = (f32[6,512]{1,0:T(8,128)S(1)}, f32[6,512]{1,0:T(8,128)S(1)}, f32[512,512]{1,0:T(8,128)}) fusion(f32[6,512]{1,0:T(8,128)} %copy-done.147, f32[512,512]{1,0:T(8,128)} %fusion.420, pred[512,512]{1,0:T(8,128)(4,1)} %copy.331, f32[6,64,512]{2,1,0:T(8,128)} %bitcast.743, f32[512,6,64]{0,2,1:T(8,128)} %bitcast.740, f32[512,6]{0,1:T(8,128)S(1)} %copy-done.123), kind=kOutput, calls=%fused_computation.784 | convolution fusion | flops 1222043648 | bytes 3981312 | tf_op jit(solution)/shard_map/transpose(jvp(hts,shp->thp))/dot_general | solution.py:549
  389.1 6.1 multiply_reduce_fusion.6
  445.4 8.6 %collective-permute-done.51 = bf16[304,1024]{1,0:T(8,128)(2,1)S(1)} collective-permute-done((bf16[304,1024]{1,0:T(8,128)(2,1)S(1)}, bf16[304,1024]{1,0:T(8,128)(2,1)S(1)}, u32[]{:S(2)}, u32[]{:S(2)}) %collective-permute-start.51) | collective-permute-done | bytes 622624 | tf_op jit(solution)/shard_map/ppermute | solution.py:139
  460.6 6.8 collective-permute-done.50
  486.7 5.9 collective-permute-done.49
  509.5 6.6 collective-permute-start.73
  518.8 9.2 %collective-permute-done.68 = bf16[272,1024]{1,0:T(8,128)(2,1)S(1)} collective-permute-done((bf16[272,1024]{1,0:T(8,128)(2,1)S(1)}, bf16[272,1024]{1,0:T(8,128)(2,1)S(1)}, u32[]{:S(2)}, u32[]{:S(2)}) %collective-permute-start.68) | collective-permute-done | bytes 557088 | tf_op jit(solution)/shard_map/ppermute | solution.py:139
  533.3 6.9 %collective-permute-start.64 = (f32[8,128]{1,0:T(8,128)S(1)}, f32[8,128]{1,0:T(8,128)S(1)}, u32[]{:S(2)}, u32[]{:S(2)}) collective-permute-start(f32[8,128]{1,0:T(8,128)S(1)} %add.979), channel_id=1, source_target_pairs={{0,8},{4,12},{8,0},{12,4},{16,24},{20,28},{24,16},{28,20},{1,9},{5... | collective-permute-start | bytes 12296 | tf_op jit(solution)/shard_map/ppermute | solution.py:43
  543.3 5.4 collective-permute-start.54
  555.7 5.7 collective-permute-start.65
  561.6 10.4 %collective-permute-done.74 = bf16[272,1024]{1,0:T(8,128)(2,1)S(1)} collective-permute-done((bf16[272,1024]{1,0:T(8,128)(2,1)S(1)}, bf16[272,1024]{1,0:T(8,128)(2,1)S(1)}, u32[]{:S(2)}, u32[]{:S(2)}) %collective-permute-start.74) | collective-permute-done | bytes 557088 | tf_op jit(solution)/shard_map/ppermute | solution.py:147
  572.1 15.6 %conditional.7 = (f32[2,2,1537,128]{3,2,1,0:T(8,128)}) conditional(s32[]{:T(128)} %clamp.2, (s32[]{:T(128)}, bf16[8,272,1024]{2,1,0:T(8,128)(2,1)}, s32[]{:T(128)}, f32[272,1024]{1,0:T(8,128)S(1)}, f32[272,1024]{1,0:T(8,128)S(1)}, /*index=5*/f32[272,1024]{1,0:T(8,128)S(1)}) %tuple.372, (s32[]{:T(128)}, ...), branch_computations={%region_45.46_spmd, %region_46.47_spmd, %region_47.48_spmd, %regio... | conditional | flops 3736580 | bytes 44544060 | solution.py:431
  589.2 6.5 copy.418
  597.8 34.9 %conditional.6 = (f32[2,2,1545,128]{3,2,1,0:T(8,128)}) conditional(s32[]{:T(128)} %clamp.2, (s32[]{:T(128)}, f32[304,1024]{1,0:T(8,128)S(1)}) %tuple.150, (s32[]{:T(128)}, f32[304,1024]{1,0:T(8,128)S(1)}) %tuple.150, (s32[]{:T(128)}, f32[304,1024]{1,0:T(8,128)S(1)}) %tuple.150, (s32[]{:T(128)}, ...), branch_computations={%region_36.37_spmd, %region_37.38_spmd, %region_38.39_spmd, %regio... | conditional | flops 3508762 | bytes 43399432 | solution.py:437
  634.3 5.7 copy.417
  640.8 5.9 bitcast_add_fusion.1
  658.7 8.5 %multiply_subtract_fusion.1 = (f32[1,196736]{1,0:T(1,128)}, f32[1,196736]{1,0:T(1,128)}, f32[1,196736]{1,0:T(1,128)}, f32[1,196736]{1,0:T(1,128)}) fusion(f32[1,196736]{1,0:T(1,128)S(1)} %copy-done.17, f32[1,196736]{1,0:T(1,128)S(1)} %copy-done.46, f32[1,196736]{1,0:T(1,128)S(1)} %copy-done.47, bf16[1,1537,128]{2,1,0:T(8,128)(2,1)S(1)} %collective-permute-done.82, ...), kind=kLoop, calls=%fused_computation.992 | loop fusion | flops 3344512 | bytes 6689028 | tf_op jit(solution)/shard_map/sub | solution.py:558
  667.4 12.1 %multiply_subtract_fusion = (f32[1,197760]{1,0:T(1,128)}, f32[1,197760]{1,0:T(1,128)}, f32[1,197760]{1,0:T(1,128)}, f32[1,197760]{1,0:T(1,128)}) fusion(f32[1,197760]{1,0:T(1,128)S(1)} %copy-done.16, f32[1,197760]{1,0:T(1,128)S(1)} %copy-done.44, f32[1,197760]{1,0:T(1,128)S(1)} %copy-done.45, bf16[1,1545,128]{2,1,0:T(8,128)(2,1)S(1)} %collective-permute-done.67, ...), kind=kLoop, calls=%fused_computation.980 | loop fusion | flops 3361920 | bytes 6723844 | tf_op jit(solution)/shard_map/sub | solution.py:558
  (883 shorter events, 403.0 us)
Async XLA Ops:
  0.7 26.7 %collective-permute-start.15 = (s32[1,1,128]{2,1,0:T(1,128)}, s32[1,1,128]{2,1,0:T(1,128)S(1)}, u32[]{:S(2)}, u32[]{:S(2)}) collective-permute-start(s32[1,1,128]{2,1,0:T(1,128)} %bitcast.764), channel_id=1, source_target_pairs={{0,2},{1,3},{2,0},{3,1},{4,6},{5,7},{6,4},{7,5},{8,10},{9,11},{10,... | collective-permute-start | bytes 1544 | tf_op jit(solution)/shard_map/ppermute | solution.py:43
  5.5 98.1 %collective-permute-start.40 = (bf16[1,128,1024]{2,1,0:T(8,128)(2,1)}, bf16[1,128,1024]{2,1,0:T(8,128)(2,1)}, u32[]{:S(2)}, u32[]{:S(2)}) collective-permute-start(bf16[1,128,1024]{2,1,0:T(8,128)(2,1)} %convert_bitcast_fusion.1), channel_id=1, source_target_pairs={{0,2},{1,3},{2,0},{3,1},{4,6},{5,7},{6,4},{7,5},{8,10},{9,11},{10,... | collective-permute-start | bytes 786440 | tf_op jit(solution)/shard_map/ppermute | solution.py:43
  47.0 27.5 %collective-permute-start.1 = (bf16[2,1545,128]{2,0,1:T(2,128)(2,1)}, bf16[2,1545,128]{2,0,1:T(2,128)(2,1)}, u32[]{:S(2)}, u32[]{:S(2)}) collective-permute-start(bf16[2,1545,128]{2,0,1:T(2,128)(2,1)} %copy.324), channel_id=1, source_target_pairs={{0,1},{1,0},{2,3},{3,2},{4,5},{5,4},{6,7},{7,6},{8,9},{9,8},{10,11... | collective-permute-start | bytes 2373128 | tf_op jit(solution)/shard_map/ppermute | solution.py:43
  65.7 39.6 %collective-permute-start.30 = (bf16[272,1024]{1,0:T(8,128)(2,1)}, bf16[272,1024]{1,0:T(8,128)(2,1)}, u32[]{:S(2)}, u32[]{:S(2)}) collective-permute-start(bf16[272,1024]{1,0:T(8,128)(2,1)} %get-tuple-element.799), channel_id=1, source_target_pairs={{8,0},{12,4},{16,8},{20,12},{24,16},{28,20},{9,1},{13,5},{17,9},{2... | collective-permute-start | bytes 1671176 | tf_op jit(solution)/shard_map/ppermute | solution.py:109
  67.0 43.7 %collective-permute-start.29 = (bf16[272,1024]{1,0:T(8,128)(2,1)}, bf16[272,1024]{1,0:T(8,128)(2,1)}, u32[]{:S(2)}, u32[]{:S(2)}) collective-permute-start(bf16[272,1024]{1,0:T(8,128)(2,1)} %get-tuple-element.799), channel_id=1, source_target_pairs={{0,4},{4,0},{8,12},{12,8},{16,20},{20,16},{24,28},{28,24},{1,5},{5... | collective-permute-start | bytes 1671176 | tf_op jit(solution)/shard_map/ppermute | solution.py:93
  69.2 42.8 %collective-permute-start.23 = (bf16[272,1024]{1,0:T(8,128)(2,1)}, bf16[272,1024]{1,0:T(8,128)(2,1)}, u32[]{:S(2)}, u32[]{:S(2)}) collective-permute-start(bf16[272,1024]{1,0:T(8,128)(2,1)} %get-tuple-element.799), channel_id=1, source_target_pairs={{0,8},{4,12},{8,16},{12,20},{16,24},{20,28},{1,9},{5,13},{9,17},{1... | collective-permute-start | bytes 1671176 | tf_op jit(solution)/shard_map/ppermute | solution.py:108
  121.7 24.1 %collective-permute-start.10 = (bf16[304,1024]{1,0:T(8,128)(2,1)S(1)}, bf16[304,1024]{1,0:T(8,128)(2,1)S(1)}, u32[]{:S(2)}, u32[]{:S(2)}) collective-permute-start(bf16[304,1024]{1,0:T(8,128)(2,1)S(1)} %collective-permute-done.9), channel_id=1, source_target_pairs={{0,4},{4,0},{8,12},{12,8},{16,20},{20,16},{1,5},{5,1},{9,13},{13,9... | collective-permute-start | bytes 1867784 | tf_op jit(solution)/shard_map/ppermute | solution.py:93
  151.7 48.8 %collective-permute-start.13 = (bf16[304,1024]{1,0:T(8,128)(2,1)S(1)}, bf16[304,1024]{1,0:T(8,128)(2,1)S(1)}, u32[]{:S(2)}, u32[]{:S(2)}) collective-permute-start(bf16[304,1024]{1,0:T(8,128)(2,1)S(1)} %collective-permute-done.11), channel_id=1, source_target_pairs={{8,0},{12,4},{9,1},{13,5},{10,2},{14,6},{11,3},{15,7}} | collective-permute-start | bytes 1867784 | tf_op jit(solution)/shard_map/ppermute | solution.py:109
  157.7 45.4 %collective-permute-start.6 = (bf16[304,1024]{1,0:T(8,128)(2,1)S(1)}, bf16[304,1024]{1,0:T(8,128)(2,1)S(1)}, u32[]{:S(2)}, u32[]{:S(2)}) collective-permute-start(bf16[304,1024]{1,0:T(8,128)(2,1)S(1)} %collective-permute-done.3), channel_id=1, source_target_pairs={{16,20},{20,16},{24,28},{28,24},{17,21},{21,17},{25,29},{29,25},{1... | collective-permute-start | bytes 1867784 | tf_op jit(solution)/shard_map/ppermute | solution.py:93
  158.5 47.8 %collective-permute-start.4 = (bf16[304,1024]{1,0:T(8,128)(2,1)S(1)}, bf16[304,1024]{1,0:T(8,128)(2,1)S(1)}, u32[]{:S(2)}, u32[]{:S(2)}) collective-permute-start(bf16[304,1024]{1,0:T(8,128)(2,1)S(1)} %collective-permute-done.3), channel_id=1, source_target_pairs={{16,24},{20,28},{17,25},{21,29},{18,26},{22,30},{19,27},{23,31}} | collective-permute-start | bytes 1867784 | tf_op jit(solution)/shard_map/ppermute | solution.py:108
  160.3 40.1 %collective-permute-start.34 = (bf16[272,1024]{1,0:T(8,128)(2,1)S(1)}, bf16[272,1024]{1,0:T(8,128)(2,1)}, u32[]{:S(2)}, u32[]{:S(2)}) collective-permute-start(bf16[272,1024]{1,0:T(8,128)(2,1)S(1)} %collective-permute-done.32), channel_id=1, source_target_pairs={{8,0},{12,4},{9,1},{13,5},{10,2},{14,6},{11,3},{15,7}} | collective-permute-start | bytes 1671176 | tf_op jit(solution)/shard_map/ppermute | solution.py:109
  169.4 37.6 %collective-permute-start.26 = (bf16[272,1024]{1,0:T(8,128)(2,1)S(1)}, bf16[272,1024]{1,0:T(8,128)(2,1)S(1)}, u32[]{:S(2)}, u32[]{:S(2)}) collective-permute-start(bf16[272,1024]{1,0:T(8,128)(2,1)S(1)} %collective-permute-done.25), channel_id=1, source_target_pairs={{24,28},{28,24},{25,29},{29,25},{26,30},{30,26},{27,31},{31,27}} | collective-permute-start | bytes 1671176 | tf_op jit(solution)/shard_map/ppermute | solution.py:93
  200.4 108.5 %collective-permute-start.41 = (bf16[2,128,1024]{2,1,0:T(8,128)(2,1)}, bf16[2,128,1024]{2,1,0:T(8,128)(2,1)}, u32[]{:S(2)}, u32[]{:S(2)}) collective-permute-start(bf16[2,128,1024]{2,1,0:T(8,128)(2,1)} %maximum_bitcast_fusion.24), channel_id=1, source_target_pairs={{0,1},{1,0},{2,3},{3,2},{4,5},{5,4},{6,7},{7,6},{8,9},{9,8},{10,11... | collective-permute-start | bytes 1572872 | tf_op jit(solution)/shard_map/ppermute | solution.py:43
  200.4 96.5 %collective-permute-start.35 = (bf16[272,1024]{1,0:T(8,128)(2,1)}, bf16[272,1024]{1,0:T(8,128)(2,1)}, u32[]{:S(2)}, u32[]{:S(2)}) collective-permute-start(bf16[272,1024]{1,0:T(8,128)(2,1)} %collective-permute-done.34), channel_id=1, source_target_pairs={{0,4},{4,0},{1,5},{5,1},{2,6},{6,2},{3,7},{7,3}} | collective-permute-start | bytes 1671176 | tf_op jit(solution)/shard_map/ppermute | solution.py:93
  203.2 27.7 %collective-permute-start.14 = (bf16[304,1024]{1,0:T(8,128)(2,1)S(1)}, bf16[304,1024]{1,0:T(8,128)(2,1)S(1)}, u32[]{:S(2)}, u32[]{:S(2)}) collective-permute-start(bf16[304,1024]{1,0:T(8,128)(2,1)S(1)} %collective-permute-done.13), channel_id=1, source_target_pairs={{0,4},{4,0},{1,5},{5,1},{2,6},{6,2},{3,7},{7,3}} | collective-permute-start | bytes 1867784 | tf_op jit(solution)/shard_map/ppermute | solution.py:93
  356.1 113.5 %collective-permute-start.75 = (bf16[272,1024]{1,0:T(8,128)(2,1)}, bf16[272,1024]{1,0:T(8,128)(2,1)}, u32[]{:S(2)}, u32[]{:S(2)}) collective-permute-start(bf16[272,1024]{1,0:T(8,128)(2,1)} %get-tuple-element.631), channel_id=1, source_target_pairs={{8,12},{12,8},{16,20},{20,16},{24,28},{28,24},{9,13},{13,9},{17,21... | collective-permute-start | bytes 1671176 | tf_op jit(solution)/shard_map/ppermute | solution.py:139
  357.6 80.4 %collective-permute-start.77 = (bf16[272,1024]{1,0:T(8,128)(2,1)}, bf16[272,1024]{1,0:T(8,128)(2,1)}, u32[]{:S(2)}, u32[]{:S(2)}) collective-permute-start(bf16[272,1024]{1,0:T(8,128)(2,1)} %get-tuple-element.632), channel_id=1, source_target_pairs={{24,28},{28,24},{25,29},{29,25},{26,30},{30,26},{27,31},{31,27}} | collective-permute-start | bytes 1671176 | tf_op jit(solution)/shard_map/ppermute | solution.py:139
  359.1 97.3 %collective-permute-start.76 = (bf16[272,1024]{1,0:T(8,128)(2,1)}, bf16[272,1024]{1,0:T(8,128)(2,1)}, u32[]{:S(2)}, u32[]{:S(2)}) collective-permute-start(bf16[272,1024]{1,0:T(8,128)(2,1)} %get-tuple-element.633), channel_id=1, source_target_pairs={{16,20},{20,16},{24,28},{28,24},{17,21},{21,17},{25,29},{29,25},{1... | collective-permute-start | bytes 1671176 | tf_op jit(solution)/shard_map/ppermute | solution.py:139
  440.1 27.3 %collective-permute-start.50 = (bf16[304,1024]{1,0:T(8,128)(2,1)S(1)}, bf16[304,1024]{1,0:T(8,128)(2,1)S(1)}, u32[]{:S(2)}, u32[]{:S(2)}) collective-permute-start(bf16[304,1024]{1,0:T(8,128)(2,1)S(1)} %get-tuple-element.625), channel_id=1, source_target_pairs={{0,4},{4,0},{8,12},{12,8},{1,5},{5,1},{9,13},{13,9},{2,6},{6,2},{1... | collective-permute-start | bytes 1867784 | tf_op jit(solution)/shard_map/ppermute | solution.py:139
  479.3 25.3 %collective-permute-start.70 = (bf16[272,1024]{1,0:T(8,128)(2,1)S(1)}, bf16[272,1024]{1,0:T(8,128)(2,1)S(1)}, u32[]{:S(2)}, u32[]{:S(2)}) collective-permute-start(bf16[272,1024]{1,0:T(8,128)(2,1)S(1)} %copy-done.55), channel_id=1, source_target_pairs={{0,4},{4,0},{8,12},{12,8},{1,5},{5,1},{9,13},{13,9},{2,6},{6,2},{1... | collective-permute-start | bytes 1671176 | tf_op jit(solution)/shard_map/ppermute | solution.py:139
  482.1 26.0 %collective-permute-start.56 = (bf16[304,1024]{1,0:T(8,128)(2,1)S(1)}, bf16[304,1024]{1,0:T(8,128)(2,1)S(1)}, u32[]{:S(2)}, u32[]{:S(2)}) collective-permute-start(bf16[304,1024]{1,0:T(8,128)(2,1)S(1)} %get-tuple-element.622), channel_id=1, source_target_pairs={{16,20},{20,16},{24,28},{28,24},{17,21},{21,17},{25,29},{29,25},{1... | collective-permute-start | bytes 1867784 | tf_op jit(solution)/shard_map/ppermute | solution.py:139
  498.0 35.2 %collective-permute-start.69 = (bf16[272,1024]{1,0:T(8,128)(2,1)}, bf16[272,1024]{1,0:T(8,128)(2,1)}, u32[]{:S(2)}, u32[]{:S(2)}) collective-permute-start(bf16[272,1024]{1,0:T(8,128)(2,1)} %get-tuple-element.636), channel_id=1, source_target_pairs={{0,4},{4,0},{8,12},{12,8},{16,20},{20,16},{1,5},{5,1},{9,13},{13,9... | collective-permute-start | bytes 1671176 | tf_op jit(solution)/shard_map/ppermute | solution.py:139
  504.6 23.4 %collective-permute-start.68 = (bf16[272,1024]{1,0:T(8,128)(2,1)S(1)}, bf16[272,1024]{1,0:T(8,128)(2,1)S(1)}, u32[]{:S(2)}, u32[]{:S(2)}) collective-permute-start(bf16[272,1024]{1,0:T(8,128)(2,1)S(1)} %copy-done.54), channel_id=1, source_target_pairs={{0,4},{4,0},{8,12},{12,8},{16,20},{20,16},{24,28},{28,24},{1,5},{5... | collective-permute-start | bytes 1671176 | tf_op jit(solution)/shard_map/ppermute | solution.py:139
  505.6 37.7 %collective-permute-start.55 = (bf16[304,1024]{1,0:T(8,128)(2,1)}, bf16[304,1024]{1,0:T(8,128)(2,1)}, u32[]{:S(2)}, u32[]{:S(2)}) collective-permute-start(bf16[304,1024]{1,0:T(8,128)(2,1)} %get-tuple-element.623), channel_id=1, source_target_pairs={{8,12},{12,8},{16,20},{20,16},{24,28},{28,24},{9,13},{13,9},{17,21... | collective-permute-start | bytes 1867784 | tf_op jit(solution)/shard_map/ppermute | solution.py:139
  509.5 30.6 %collective-permute-start.73 = (bf16[272,1024]{1,0:T(8,128)(2,1)}, bf16[272,1024]{1,0:T(8,128)(2,1)}, u32[]{:S(2)}, u32[]{:S(2)}) collective-permute-start(bf16[272,1024]{1,0:T(8,128)(2,1)} %fusion.341), channel_id=1, source_target_pairs={{0,8},{4,12},{8,16},{12,20},{1,9},{5,13},{9,17},{13,21},{2,10},{6,... | collective-permute-start | bytes 1671176 | tf_op jit(solution)/shard_map/ppermute | solution.py:147
  517.3 31.4 %collective-permute-start.59 = (bf16[304,1024]{1,0:T(8,128)(2,1)}, bf16[304,1024]{1,0:T(8,128)(2,1)}, u32[]{:S(2)}, u32[]{:S(2)}) collective-permute-start(bf16[304,1024]{1,0:T(8,128)(2,1)} %fusion.312), channel_id=1, source_target_pairs={{16,8},{20,12},{24,16},{28,20},{17,9},{21,13},{25,17},{29,21},{18,... | collective-permute-start | bytes 1867784 | tf_op jit(solution)/shard_map/ppermute | solution.py:150
  532.4 63.3 %collective-permute-start.48 = (bf16[304,1024]{1,0:T(8,128)(2,1)}, bf16[304,1024]{1,0:T(8,128)(2,1)}, u32[]{:S(2)}, u32[]{:S(2)}) collective-permute-start(bf16[304,1024]{1,0:T(8,128)(2,1)} %get-tuple-element.620), channel_id=1, source_target_pairs={{0,4},{4,0},{8,12},{12,8},{16,20},{20,16},{24,28},{28,24},{1,5},{5... | collective-permute-start | bytes 1867784 | tf_op jit(solution)/shard_map/ppermute | solution.py:139
  543.3 52.4 %collective-permute-start.54 = (bf16[304,1024]{1,0:T(8,128)(2,1)}, bf16[304,1024]{1,0:T(8,128)(2,1)}, u32[]{:S(2)}, u32[]{:S(2)}) collective-permute-start(bf16[304,1024]{1,0:T(8,128)(2,1)} %get-tuple-element.627), channel_id=1, source_target_pairs={{0,8},{4,12},{8,16},{12,20},{16,24},{20,28},{1,9},{5,13},{9,17},{1... | collective-permute-start | bytes 1867784 | tf_op jit(solution)/shard_map/ppermute | solution.py:147
  548.7 23.3 %collective-permute-start.74 = (bf16[272,1024]{1,0:T(8,128)(2,1)S(1)}, bf16[272,1024]{1,0:T(8,128)(2,1)S(1)}, u32[]{:S(2)}, u32[]{:S(2)}) collective-permute-start(bf16[272,1024]{1,0:T(8,128)(2,1)S(1)} %fusion.343), channel_id=1, source_target_pairs={{0,8},{4,12},{8,16},{12,20},{16,24},{20,28},{1,9},{5,13},{9,17},{1... | collective-permute-start | bytes 1671176 | tf_op jit(solution)/shard_map/ppermute | solution.py:147
  553.3 42.3 %collective-permute-start.60 = (bf16[304,1024]{1,0:T(8,128)(2,1)}, bf16[304,1024]{1,0:T(8,128)(2,1)}, u32[]{:S(2)}, u32[]{:S(2)}) collective-permute-start(bf16[304,1024]{1,0:T(8,128)(2,1)} %fusion.314), channel_id=1, source_target_pairs={{8,0},{12,4},{16,8},{20,12},{24,16},{28,20},{9,1},{13,5},{17,9},{2... | collective-permute-start | bytes 1867784 | tf_op jit(solution)/shard_map/ppermute | solution.py:150
  555.7 42.0 %collective-permute-start.65 = (f32[8,128]{1,0:T(8,128)S(1)}, f32[8,128]{1,0:T(8,128)S(1)}, u32[]{:S(2)}, u32[]{:S(2)}) collective-permute-start(f32[8,128]{1,0:T(8,128)S(1)} %add.980), channel_id=1, source_target_pairs={{0,16},{4,20},{8,24},{12,28},{16,0},{20,4},{24,8},{28,12},{1,17},{... | collective-permute-start | bytes 12296 | tf_op jit(solution)/shard_map/ppermute | solution.py:43
  595.7 45.1 %collective-permute-start.81 = (bf16[2,1537,128]{2,0,1:T(2,128)(2,1)}, bf16[2,1537,128]{2,0,1:T(2,128)(2,1)}, u32[]{:S(2)}, u32[]{:S(2)}) collective-permute-start(bf16[2,1537,128]{2,0,1:T(2,128)(2,1)} %bitcast.677), channel_id=1, source_target_pairs={{0,1},{1,0},{2,3},{3,2},{4,5},{5,4},{6,7},{7,6},{8,9},{9,8},{10,11... | collective-permute-start | bytes 2360840 | tf_op jit(solution)/shard_map/ppermute | solution.py:43
  (206 other events, 1812.2 us)
